TPU v7x, 512 devices: a whole 4x8x8 slice. The times are simulated.
512 devices in a mesh: fib: 64 (over z, x, core), pln: 8 (over y).
Axes of the slice: x: 4, y: 8, z: 8, core: 2. Of those that a mesh axis runs over, the one named last changes fastest.
Arguments:
- nodal_values: float32 [8, 64, 288, 1000], P('pln', 'fib'), may hold values from -6 to 6
- interp_matrix: float32 [1000, 512], replicated, may hold values from -0.1875 to 0.1875
- count_table: int32 [8, 64, 3], P('pln'), may hold values from 1 to 96, as said below
- slot_order: int32 [8, 64, 192], P('pln', 'fib'), may hold values from 0 to 191, each once within a row
- start_basis: float32 [768, 128], replicated, may hold values from -6 to 6
Outputs:
- core_values: float32 [8, 64, 128, 128], P('pln', 'fib')
Inputs may be any that keep to these rules, and one draw needn't show every extreme that they name: count_table[j, o, d] elements of owner o come from the source d places before it along fib, cyclically; for every owner the 3 entries sum to 192 and one equals 96. `slot_order`: each owner's row is a permutation.
All inputs are finite; a program needn't handle non-finite values.
Results may differ from a plain program's by a relative error of at most 0.0003.
Values sent between devices are 32-bit elements; how exact they have to be, the bound alone decides.
A program may use at most 64 MiB of HBM per device.

v0:
```python
import jax
import jax.numpy as jnp
from jax import lax
from jax.sharding import PartitionSpec as P

NX = 768
TILES_DEV = 1


def shifted(value, axis, by):
    peers = lax.axis_size(axis)
    return lax.ppermute(value, axis, [(i, (i + by) % peers) for i in range(peers)])


def per_device(nodal_values, interp_matrix, count_table, slot_order, start_basis):
    full_precision = lax.Precision.HIGHEST
    node_rows = nodal_values[0, 0]
    owner_table = count_table[0]
    brick_order = slot_order[0, 0]
    owners = lax.axis_size("fib")
    own_index = lax.axis_index("fib")
    window = owner_table.shape[1]
    capacity = node_rows.shape[0] // window
    elements = brick_order.shape[0]
    tiles_total = TILES_DEV * owners
    block_width = NX // owners
    send_start = []
    running = jnp.int32(0)
    for distance in range(window):
        send_start.append(running)
        column = owner_table[:, distance]
        running = running + lax.dynamic_index_in_dim(
            column, (own_index + distance) % owners, 0, keepdims=False
        )
    own_counts = lax.dynamic_index_in_dim(owner_table, own_index, 0, keepdims=False)
    positions = jnp.arange(elements, dtype=jnp.int32)
    combined_index = jnp.zeros((elements,), jnp.int32)
    offset = jnp.int32(0)
    for distance in range(window - 1, -1, -1):
        taken_count = own_counts[distance]
        inside = (positions >= offset) & (positions < offset + taken_count)
        combined_index = jnp.where(inside, distance * capacity + positions - offset, combined_index)
        offset = offset + taken_count
    brick_source = jnp.zeros((elements,), jnp.int32).at[brick_order].set(combined_index)
    grid_rows = jnp.dot(
        node_rows, interp_matrix, precision=full_precision, preferred_element_type=jnp.float32
    )
    received = []
    for distance in range(window):
        send_piece = lax.dynamic_slice_in_dim(grid_rows, send_start[distance], capacity, 0)
        if distance > 0:
            send_piece = shifted(send_piece, "fib", distance)
        received.append(send_piece)
    brick_values = jnp.concatenate(received, axis=0)[brick_source]
    brick_grid = brick_values.reshape(tiles_total, block_width, brick_values.shape[1] // 4)
    fibre_field = lax.all_to_all(brick_grid, "fib", split_axis=0, concat_axis=1, tiled=True)
    gram_part = jnp.einsum("txf,tyf->xy", fibre_field, fibre_field, precision=full_precision)
    gram_matrix = lax.psum(gram_part, ("fib", "pln"))
    image_matrix = jnp.dot(gram_matrix, start_basis, precision=full_precision)
    normal_matrix = jnp.dot(image_matrix.T, image_matrix, precision=full_precision)
    lower_factor = jnp.linalg.cholesky(normal_matrix)
    new_basis = jax.scipy.linalg.solve_triangular(lower_factor, image_matrix.T, lower=True).T
    core_values = jnp.einsum("xk,txf->tkf", new_basis, fibre_field, precision=full_precision)
    return core_values[None]


def solution(mesh):
    placed = (P("pln", "fib", None, None), P(), P("pln", None, None), P("pln", "fib", None), P())
    return jax.shard_map(
        per_device,
        mesh=mesh,
        in_specs=placed,
        out_specs=P("pln", "fib", None, None),
        check_vma=False,
    )
```

profile of v0, /device:TPU:1, one launch (start us, length us, event | category | flops | bytes accessed | tf_op | source)
XLA Modules:
  0.0 377.7 jit_solution(10091446328949841219)
XLA Ops:
  6.5 0.0 copy-start
  6.5 0.0 all-reduce.2.cloned.1.call-start
  6.5 0.8 copy.12
  7.4 0.7 constant_dynamic-slice_fusion.4
  11.2 0.0 copy-done
  11.2 0.0 copy-start.2
  11.2 0.0 copy-start.3
  11.2 3.4 fusion
  14.7 0.1 fusion.8
  14.7 3.9 %collective-permute-start.1 = (f32[96,512]{1,0:T(8,128)S(1)}, f32[96,512]{1,0:T(8,128)S(1)}, u32[]{:S(2)}, u32[]{:S(2)}) collective-permute-start(f32[96,512]{1,0:T(8,128)S(1)} %get-tuple-element.6), channel_id=1, source_target_pairs={{0,16},{8,24},{16,32},{24,40},{32,48},{40,56},{48,64},{56,72},{64,... | collective-permute-start | bytes 589832 | tf_op jit(solution)/shard_map/ppermute | solution.py:12
  18.7 4.0 %collective-permute-start = (f32[96,512]{1,0:T(8,128)S(1)}, f32[96,512]{1,0:T(8,128)S(1)}, u32[]{:S(2)}, u32[]{:S(2)}) collective-permute-start(f32[96,512]{1,0:T(8,128)S(1)} %get-tuple-element.7), channel_id=1, source_target_pairs={{0,8},{8,16},{16,24},{24,32},{32,40},{40,48},{48,56},{56,64},{64,7... | collective-permute-start | bytes 589832 | tf_op jit(solution)/shard_map/ppermute | solution.py:12
  22.6 0.0 copy-done.2
  22.6 0.7 constant_dynamic-slice_fusion.2
  25.2 0.6 and_select_fusion.1
  25.8 0.0 copy-done.3
  25.8 1.2 scatter_custom_fusion
  27.1 5.9 %collective-permute-done.1 = f32[96,512]{1,0:T(8,128)S(1)} collective-permute-done((f32[96,512]{1,0:T(8,128)S(1)}, f32[96,512]{1,0:T(8,128)S(1)}, u32[]{:S(2)}, u32[]{:S(2)}) %collective-permute-start.1) | collective-permute-done | bytes 196640 | tf_op jit(solution)/shard_map/ppermute | solution.py:12
  33.0 0.0 collective-permute-done
  33.0 0.9 gather_fusion
  33.9 0.1 reshape.65
  34.0 25.5 %all_to_all.4 = f32[64,12,128]{2,1,0:T(8,128)S(1)} all-to-all(f32[64,12,128]{2,1,0:T(8,128)S(1)} %reshape.65), channel_id=1, replica_groups=mesh['fib'=64,'pln'=8] {'fib'}, dimensions={0} | all-to-all | bytes 786432 | tf_op jit(solution)/shard_map/all_to_all | solution.py:56
  59.6 0.0 copy-start.1
  59.6 3.4 fusion.10
  63.0 0.0 all-reduce.2.cloned.1.call-update
  63.0 278.3 %all-reduce.2.cloned.1.call-done = f32[768,768]{1,0:T(8,128)} async-done(((f32[768,768]{1,0:T(8,128)}), f32[768,768]{1,0:T(8,128)}) %all-reduce.2.cloned.1.call-update) | async-done | bytes 2359312 | tf_op jit(solution)/shard_map/psum | solution.py:58
  341.3 0.0 copy-done.1
  341.3 3.7 fusion.11
  345.0 0.8 fusion.12
  345.8 0.1 copy.8
  345.9 11.7 %cholesky.16 = f32[128,128]{1,0:T(8,128)S(1)} custom-call(f32[128,128]{1,0:T(8,128)S(1)} %fusion.5), custom_call_target="Cholesky" | custom-call | tf_op jit(solution)/shard_map/jit(cholesky)/cholesky | solution.py:61
  357.7 0.6 compare_reduce_fusion
  358.3 0.7 fusion.2
  359.0 9.8 %custom-call.7 = f32[1,128,128]{1,2,0:T(8,128)S(1)} custom-call(f32[1,128,128]{2,1,0:T(8,128)S(1)} %fusion.2), custom_call_target="InvertDiagBlocksLowerTriangular" | custom-call | tf_op jit(solution)/shard_map/jit(_solve_triangular)/triangular_solve | solution.py:62
  368.8 0.5 fusion.3
  369.3 0.8 convolution_bitcast_fusion
  370.1 0.7 copy.9
  (8 shorter events, 0.1 us)
Async XLA Ops:
  6.5 4.7 %copy-start = (f32[1000,512]{1,0:T(8,128)S(1)}, f32[1000,512]{1,0:T(8,128)}, u32[]{:S(2)}) copy-start(f32[1000,512]{1,0:T(8,128)} %param.6) | copy-start | bytes 6144004
  6.5 334.8 %all-reduce.2.cloned.1.call-start = ((), (), s32[]{:S(2)}) async-start(), calls=%async_computation.1 | async-start | bytes 4718592 | tf_op jit(solution)/shard_map/psum | solution.py:58
  11.2 11.4 %copy-start.2 = (s32[1,64,3]{1,0,2:T(1,128)S(1)}, s32[1,64,3]{1,0,2:T(1,128)}, u32[]{:S(2)}) copy-start(s32[1,64,3]{1,0,2:T(1,128)} %param.7) | copy-start | bytes 2308
  11.2 14.6 %copy-start.3 = (s32[1,1,192]{2,1,0:T(1,128)S(1)}, s32[1,1,192]{2,1,0:T(1,128)}, u32[]{:S(2)}) copy-start(s32[1,1,192]{2,1,0:T(1,128)} %param.8) | copy-start | bytes 2308
  14.7 18.3 %collective-permute-start.1 = (f32[96,512]{1,0:T(8,128)S(1)}, f32[96,512]{1,0:T(8,128)S(1)}, u32[]{:S(2)}, u32[]{:S(2)}) collective-permute-start(f32[96,512]{1,0:T(8,128)S(1)} %get-tuple-element.6), channel_id=1, source_target_pairs={{0,16},{8,24},{16,32},{24,40},{32,48},{40,56},{48,64},{56,72},{64,... | collective-permute-start | bytes 589832 | tf_op jit(solution)/shard_map/ppermute | solution.py:12
  18.7 14.3 %collective-permute-start = (f32[96,512]{1,0:T(8,128)S(1)}, f32[96,512]{1,0:T(8,128)S(1)}, u32[]{:S(2)}, u32[]{:S(2)}) collective-permute-start(f32[96,512]{1,0:T(8,128)S(1)} %get-tuple-element.7), channel_id=1, source_target_pairs={{0,8},{8,16},{16,24},{24,32},{32,40},{40,48},{48,56},{56,64},{64,7... | collective-permute-start | bytes 589832 | tf_op jit(solution)/shard_map/ppermute | solution.py:12
  59.6 281.8 %copy-start.1 = (f32[768,128]{1,0:T(8,128)S(1)}, f32[768,128]{1,0:T(8,128)}, u32[]{:S(2)}) copy-start(f32[768,128]{1,0:T(8,128)} %param.9) | copy-start | bytes 1179652
Sparse Core Ops, SparseCore 0:
  63.1 278.1 all-reduce.1
where the time goes:
time: 378 us
  waiting for transfers between devices  284 us (75%)
  blocking collectives  25.5 us (7%)
  other arithmetic  23.5 us (6%)
  between operations  18.7 us (5%)
  matrix products  12.6 us (3%)
  starting transfers between devices  7.9 us (2%)
  local copies, waits for them, and re-layouts  5.23 us (1%)
    psum x1, waiting for transfers between devices, per_device(): gram_matrix = lax.psum(gram_part, ('fib', 'pln'))  278 us
    all_to_all x1, blocking collectives, per_device(): lax.all_to_all(brick_grid, 'fib', split_axis=0, concat_axis=1, tiled=True)  25.5 us
    another operation x3, other arithmetic, per_device(): lower_factor = jnp.linalg.cholesky(normal_matrix)  12.4 us
    another operation x2, other arithmetic, per_device(): jax.scipy.linalg.solve_triangular(lower_factor, image_matrix.T, lower=True)  10.5 us
    ppermute x2, starting transfers between devices, shifted(): lax.ppermute(value, axis, [(i, (i + by) % peers) for i in range(peers)])  7.9 us
  transfers between devices with their start and end apart: 3, of which 2 were waited for; matrix products, arithmetic and copies ran while one was open for 1% of the time, Pallas kernels for 0%

commit v1 on v0

--- a/solution.py
+++ b/solution.py
@@ -1,10 +1,15 @@
+import functools
+
 import jax
 import jax.numpy as jnp
 from jax import lax
+from jax.experimental import pallas as pl
+from jax.experimental.pallas import tpu as pltpu
 from jax.sharding import PartitionSpec as P
 
 NX = 768
-TILES_DEV = 1
+RANK = 128
+HIGHEST = lax.Precision.HIGHEST
 
 
 def shifted(value, axis, by):
@@ -12,8 +17,38 @@
     return lax.ppermute(value, axis, [(i, (i + by) % peers) for i in range(peers)])
 
 
+def eliminate_kernel(normal_ref, right_ref, out_ref):
+    blocks = RANK // 8
+    left = [normal_ref[8 * m:8 * m + 8, :] for m in range(blocks)]
+    right = [right_ref[8 * m:8 * m + 8, :] for m in range(blocks)]
+    rows = lax.broadcasted_iota(jnp.int32, (8, RANK), 0)
+    for k in range(RANK):
+        i, r = divmod(k, 8)
+        row_left = left[i][r:r + 1, :]
+        row_right = right[i][r:r + 1, :]
+        pivot = row_left[:, k:k + 1]
+        inverse = 1.0 / pivot
+        scaled_left = row_left * inverse
+        scaled_right = row_right * inverse
+        out_ref[k:k + 1, :] = row_right * lax.rsqrt(pivot)
+        for m in range(i, blocks):
+            factor = jnp.broadcast_to(left[m][:, k:k + 1], (8, RANK))
+            if m == i:
+                factor = jnp.where(rows > r, factor, 0.0)
+            left[m] = left[m] - factor * scaled_left
+            right[m] = right[m] - factor * scaled_right
+
+
+def eliminate(normal, right):
+    return pl.pallas_call(
+        eliminate_kernel,
+        out_shape=jax.ShapeDtypeStruct((RANK, right.shape[1]), jnp.float32),
+        in_specs=[pl.BlockSpec(memory_space=pltpu.VMEM)] * 2,
+        out_specs=pl.BlockSpec(memory_space=pltpu.VMEM),
+    )(normal, right)
+
+
 def per_device(nodal_values, interp_matrix, count_table, slot_order, start_basis):
-    full_precision = lax.Precision.HIGHEST
     node_rows = nodal_values[0, 0]
     owner_table = count_table[0]
     brick_order = slot_order[0, 0]
@@ -22,7 +57,6 @@
     window = owner_table.shape[1]
     capacity = node_rows.shape[0] // window
     elements = brick_order.shape[0]
-    tiles_total = TILES_DEV * owners
     block_width = NX // owners
     send_start = []
     running = jnp.int32(0)
@@ -43,7 +77,7 @@
         offset = offset + taken_count
     brick_source = jnp.zeros((elements,), jnp.int32).at[brick_order].set(combined_index)
     grid_rows = jnp.dot(
-        node_rows, interp_matrix, precision=full_precision, preferred_element_type=jnp.float32
+        node_rows, interp_matrix, precision=HIGHEST, preferred_element_type=jnp.float32
     )
     received = []
     for distance in range(window):
@@ -52,16 +86,15 @@
             send_piece = shifted(send_piece, "fib", distance)
         received.append(send_piece)
     brick_values = jnp.concatenate(received, axis=0)[brick_source]
-    brick_grid = brick_values.reshape(tiles_total, block_width, brick_values.shape[1] // 4)
+    brick_grid = brick_values.reshape(owners, block_width, brick_values.shape[1] // 4)
     fibre_field = lax.all_to_all(brick_grid, "fib", split_axis=0, concat_axis=1, tiled=True)
-    gram_part = jnp.einsum("txf,tyf->xy", fibre_field, fibre_field, precision=full_precision)
-    gram_matrix = lax.psum(gram_part, ("fib", "pln"))
-    image_matrix = jnp.dot(gram_matrix, start_basis, precision=full_precision)
-    normal_matrix = jnp.dot(image_matrix.T, image_matrix, precision=full_precision)
-    lower_factor = jnp.linalg.cholesky(normal_matrix)
-    new_basis = jax.scipy.linalg.solve_triangular(lower_factor, image_matrix.T, lower=True).T
-    core_values = jnp.einsum("xk,txf->tkf", new_basis, fibre_field, precision=full_precision)
-    return core_values[None]
+    field = fibre_field[0]
+    coefficients = jnp.einsum("xf,xk->fk", field, start_basis, precision=HIGHEST)
+    image = lax.psum(jnp.dot(field, coefficients, precision=HIGHEST), ("fib", "pln"))
+    normal = jnp.einsum("xk,xl->kl", image, image, precision=HIGHEST)
+    right = jnp.einsum("xk,xf->kf", image, field, precision=HIGHEST)
+    core_values = eliminate(normal, right)
+    return core_values[None, None]
 
 
 def solution(mesh):

time: 378 us -> 353 us (0.934)
  other arithmetic: 23.5 us -> 0.68 us
  Pallas kernels: 0 us -> 12.2 us
  waiting for transfers between devices: 284 us -> 275 us
    another operation x5 -> x0, other arithmetic: 22.9 us -> none  [the longest x3 12.4 us: per_device(): lower_factor = jnp.linalg.cholesky(normal_matrix)]
    pallas_call x0 -> x1, Pallas kernels: none -> 12.2 us  [eliminate(): pl.pallas_call(eliminate_kernel, out_shape=jax.ShapeDtypeStruct((RANK, ri...]
    psum x1, waiting for transfers between devices: 278 us -> 267 us  [per_device(): lax.psum(jnp.dot(field, coefficients, precision=HIGHEST), ('fib', 'pln'))]
where the time goes in v1:
time: 353 us
  waiting for transfers between devices  275 us (78%)
  blocking collectives  23.6 us (7%)
  between operations  18.9 us (5%)
  Pallas kernels  12.2 us (3%)
  matrix products  10.4 us (3%)
  starting transfers between devices  7.62 us (2%)
  local copies, waits for them, and re-layouts  4.42 us (1%)
    psum x1, waiting for transfers between devices, per_device(): lax.psum(jnp.dot(field, coefficients, precision=HIGHEST), ('fib', 'pln'))  267 us
    all_to_all x1, blocking collectives, per_device(): lax.all_to_all(brick_grid, 'fib', split_axis=0, concat_axis=1, tiled=True)  23.6 us
    pallas_call x1, Pallas kernels, eliminate(): pl.pallas_call(eliminate_kernel, out_shape=jax.ShapeDtypeStruct((RANK, ri...  12.2 us
    ppermute x2, waiting for transfers between devices, shifted(): lax.ppermute(value, axis, [(i, (i + by) % peers) for i in range(peers)])  8.4 us
    ppermute x2, starting transfers between devices, shifted(): lax.ppermute(value, axis, [(i, (i + by) % peers) for i in range(peers)])  7.62 us
  transfers between devices with their start and end apart: 3, of which 2 were waited for; matrix products, arithmetic and copies ran while one was open for 1% of the time, Pallas kernels for 0%

profile of v1, /device:TPU:1, one launch (start us, length us, event | category | flops | bytes accessed | tf_op | source)
XLA Modules:
  0.0 352.9 jit_solution(13675175055979816167)
XLA Ops:
  6.5 0.0 copy-start
  6.5 0.0 all-reduce.2.cloned.1.call-start
  6.5 0.8 copy.8
  7.4 0.7 constant_dynamic-slice_fusion.4
  11.4 0.0 copy-done
  11.4 0.0 copy-start.2
  11.4 0.0 copy-start.3
  11.4 3.4 fusion
  14.9 0.1 fusion.4
  14.9 4.5 %collective-permute-start = (f32[96,512]{1,0:T(8,128)S(1)}, f32[96,512]{1,0:T(8,128)S(1)}, u32[]{:S(2)}, u32[]{:S(2)}) collective-permute-start(f32[96,512]{1,0:T(8,128)S(1)} %get-tuple-element.7), channel_id=1, source_target_pairs={{0,8},{8,16},{16,24},{24,32},{32,40},{40,48},{48,56},{56,64},{64,7... | collective-permute-start | bytes 589832 | tf_op jit(solution)/shard_map/ppermute | solution.py:17
  19.4 3.1 collective-permute-start.1
  22.6 0.0 copy-done.2
  22.6 0.7 constant_dynamic-slice_fusion.2
  25.2 0.6 and_select_fusion.1
  25.8 0.0 copy-done.3
  25.8 1.2 scatter_custom_fusion
  27.1 0.0 collective-permute-done
  27.1 8.4 %collective-permute-done.1 = f32[96,512]{1,0:T(8,128)S(1)} collective-permute-done((f32[96,512]{1,0:T(8,128)S(1)}, f32[96,512]{1,0:T(8,128)S(1)}, u32[]{:S(2)}, u32[]{:S(2)}) %collective-permute-start.1) | collective-permute-done | bytes 196640 | tf_op jit(solution)/shard_map/ppermute | solution.py:17
  35.5 0.9 gather_fusion
  36.4 0.0 copy-start.1
  36.4 0.1 reshape.47
  36.5 23.6 %all_to_all.4 = f32[64,12,128]{2,1,0:T(8,128)S(1)} all-to-all(f32[64,12,128]{2,1,0:T(8,128)S(1)} %reshape.47), channel_id=1, replica_groups=mesh['fib'=64,'pln'=8] {'fib'}, dimensions={0} | all-to-all | bytes 786432 | tf_op jit(solution)/shard_map/all_to_all | solution.py:90
  60.2 0.0 copy-done.1
  60.2 0.8 fusion.6
  61.0 1.2 fusion.7
  62.2 0.0 all-reduce.2.cloned.1.call-update
  62.2 266.7 %all-reduce.2.cloned.1.call-done = f32[768,128]{1,0:T(8,128)} async-done(((f32[768,128]{1,0:T(8,128)}), f32[768,128]{1,0:T(8,128)}) %all-reduce.2.cloned.1.call-update) | async-done | bytes 393232 | tf_op jit(solution)/shard_map/psum | solution.py:93
  328.9 2.4 fusion.9.right_ref
  331.3 2.5 fusion.8.normal_ref
  333.8 12.2 %shard_map.55 = f32[128,128]{1,0:T(8,128)} custom-call(f32[128,128]{1,0:T(8,128)} %fusion.8.normal_ref, f32[128,128]{1,0:T(8,128)} %fusion.9.right_ref), custom_call_target="tpu_custom_call" | custom-call | tf_op jit(solution)/shard_map/pallas_call | solution.py:43
  (6 shorter events, 0.1 us)
Async XLA Ops:
  6.5 4.9 %copy-start = (f32[1000,512]{1,0:T(8,128)S(1)}, f32[1000,512]{1,0:T(8,128)}, u32[]{:S(2)}) copy-start(f32[1000,512]{1,0:T(8,128)} %param.6) | copy-start | bytes 6144004
  6.5 322.3 %all-reduce.2.cloned.1.call-start = ((), (), s32[]{:S(2)}) async-start(), calls=%async_computation.1 | async-start | bytes 786432 | tf_op jit(solution)/shard_map/psum | solution.py:93
  11.4 11.1 %copy-start.2 = (s32[1,64,3]{1,0,2:T(1,128)S(1)}, s32[1,64,3]{1,0,2:T(1,128)}, u32[]{:S(2)}) copy-start(s32[1,64,3]{1,0,2:T(1,128)} %param.7) | copy-start | bytes 2308
  11.4 14.4 %copy-start.3 = (s32[1,1,192]{2,1,0:T(1,128)S(1)}, s32[1,1,192]{2,1,0:T(1,128)}, u32[]{:S(2)}) copy-start(s32[1,1,192]{2,1,0:T(1,128)} %param.8) | copy-start | bytes 2308
  14.9 12.2 %collective-permute-start = (f32[96,512]{1,0:T(8,128)S(1)}, f32[96,512]{1,0:T(8,128)S(1)}, u32[]{:S(2)}, u32[]{:S(2)}) collective-permute-start(f32[96,512]{1,0:T(8,128)S(1)} %get-tuple-element.7), channel_id=1, source_target_pairs={{0,8},{8,16},{16,24},{24,32},{32,40},{40,48},{48,56},{56,64},{64,7... | collective-permute-start | bytes 589832 | tf_op jit(solution)/shard_map/ppermute | solution.py:17
  19.4 16.1 %collective-permute-start.1 = (f32[96,512]{1,0:T(8,128)S(1)}, f32[96,512]{1,0:T(8,128)S(1)}, u32[]{:S(2)}, u32[]{:S(2)}) collective-permute-start(f32[96,512]{1,0:T(8,128)S(1)} %get-tuple-element.6), channel_id=1, source_target_pairs={{0,16},{8,24},{16,32},{24,40},{32,48},{40,56},{48,64},{56,72},{64,... | collective-permute-start | bytes 589832 | tf_op jit(solution)/shard_map/ppermute | solution.py:17
  36.4 23.8 %copy-start.1 = (f32[768,128]{1,0:T(8,128)S(1)}, f32[768,128]{1,0:T(8,128)}, u32[]{:S(2)}) copy-start(f32[768,128]{1,0:T(8,128)} %param.9) | copy-start | bytes 1179652
Sparse Core Ops, SparseCore 0:
  62.3 266.4 all-reduce.1

commit v2 on v1

--- a/solution.py
+++ b/solution.py
@@ -46,6 +46,165 @@
         in_specs=[pl.BlockSpec(memory_space=pltpu.VMEM)] * 2,
         out_specs=pl.BlockSpec(memory_space=pltpu.VMEM),
     )(normal, right)
+
+
+MESH_ID = pl.DeviceIdType.MESH
+X_CHIPS = 4
+
+
+class Place:
+    def __init__(self, fib_size, pln_size):
+        self.chips = fib_size // 2
+        self.planes = pln_size
+        self.fib = lax.axis_index("fib")
+        self.pln = lax.axis_index("pln")
+        self.core = lax.rem(self.fib, 2)
+        self.chip = lax.div(self.fib, 2)
+        self.z = lax.div(self.chip, X_CHIPS)
+        self.x = lax.rem(self.chip, X_CHIPS)
+
+    def other_core(self):
+        return {"fib": self.chip * 2 + 1 - self.core, "pln": self.pln}
+
+    def chip_at(self, step):
+        z = lax.rem(self.z + lax.div(step, X_CHIPS), self.chips // X_CHIPS)
+        x = lax.rem(self.x + lax.rem(step, X_CHIPS), X_CHIPS)
+        return z * X_CHIPS + x
+
+    def chip_before(self, step):
+        depth = self.chips // X_CHIPS
+        z = lax.rem(self.z + depth - lax.div(step, X_CHIPS), depth)
+        x = lax.rem(self.x + X_CHIPS - lax.rem(step, X_CHIPS), X_CHIPS)
+        return z * X_CHIPS + x
+
+    def on_chip(self, chip):
+        return {"fib": chip * 2 + self.core, "pln": self.pln}
+
+    def in_plane(self, step):
+        return {"fib": self.fib, "pln": lax.rem(self.pln + step, self.planes)}
+
+
+def remote(src, dst, send_sem, recv_sem, device):
+    return pltpu.make_async_remote_copy(
+        src_ref=src, dst_ref=dst, send_sem=send_sem, recv_sem=recv_sem,
+        device_id=device, device_id_type=MESH_ID,
+    )
+
+
+def loop(low, high, body):
+    def step(i, carry):
+        body(i)
+        return carry
+    lax.fori_loop(low, high, step, 0)
+
+
+def reduce_kernel(fib_size, pln_size, field_ref, basis_ref, image_ref, part, other, half, chip_parts,
+                  chunk_sum, plane_parts, chunk_done, core_sems, chip_send, chip_recv, plane_send,
+                  plane_recv, gather_send, gather_recv, relay_send, relay_recv):
+    at = Place(fib_size, pln_size)
+    chips, planes = at.chips, at.planes
+    size = NX // 4 // 2 // chips
+    split = size * chips
+    barrier = pltpu.get_barrier_semaphore()
+
+    def greet(device):
+        pl.semaphore_signal(barrier, inc=1, device_id=device, device_id_type=MESH_ID)
+
+    greet(at.other_core())
+    loop(1, chips, lambda i: greet(at.on_chip(at.chip_at(i))))
+    loop(1, planes, lambda i: greet(at.in_plane(i)))
+
+    field = field_ref[...]
+    coefficients = lax.dot_general(
+        field, basis_ref[...], (((0,), (0,)), ((), ())), precision=HIGHEST,
+        preferred_element_type=jnp.float32)
+    product = jnp.dot(field, coefficients, precision=HIGHEST, preferred_element_type=jnp.float32)
+    part[...] = product.reshape(NX // 4, 4, RANK)
+
+    pl.semaphore_wait(barrier, chips + planes - 1)
+
+    swap = remote(part.at[pl.ds((1 - at.core) * split, split)], other, core_sems.at[0], core_sems.at[1],
+                  at.other_core())
+    swap.start()
+    swap.wait()
+    half[...] = part[pl.ds(at.core * split, split)] + other[...]
+
+    def send_chunk(i):
+        chip = at.chip_at(i)
+        remote(half.at[pl.ds(chip * size, size)], chip_parts.at[i], chip_send.at[i], chip_recv.at[i],
+               at.on_chip(chip)).start()
+
+    def chunk_copy(i):
+        return remote(half.at[pl.ds(0, size)], chip_parts.at[i], chip_send.at[i], chip_recv.at[i],
+                      at.on_chip(at.chip_at(i)))
+
+    loop(1, chips, send_chunk)
+    chunk_sum[...] = half[pl.ds(at.chip * size, size)]
+
+    def add_chunk(i):
+        chunk_copy(i).wait_recv()
+        chunk_sum[...] += chip_parts[i]
+
+    loop(1, chips, add_chunk)
+
+    def plane_copy(i):
+        return remote(chunk_sum, plane_parts.at[i], plane_send.at[i], plane_recv.at[i], at.in_plane(i))
+
+    loop(1, planes, lambda i: plane_copy(i).start())
+    chunk_done[...] = chunk_sum[...]
+
+    def add_plane(i):
+        plane_copy(i).wait_recv()
+        chunk_done[...] += plane_parts[i]
+
+    loop(1, planes, add_plane)
+
+    def place_of(chip):
+        return pl.ds(at.core * split + chip * size, size)
+
+    def gather_copy(i):
+        return remote(chunk_done, image_ref.at[place_of(at.chip)], gather_send.at[i], gather_recv.at[i],
+                      at.on_chip(at.chip_at(i)))
+
+    def relay_copy(i, source):
+        return remote(source, image_ref.at[place_of(at.chip_before(i))], relay_send.at[i], relay_recv.at[i],
+                      at.other_core())
+
+    loop(1, chips, lambda i: gather_copy(i).start())
+    relay_copy(0, chunk_done).start()
+    image_ref[place_of(at.chip)] = chunk_done[...]
+
+    def pass_on(i):
+        gather_copy(i).wait_recv()
+        relay_copy(i, image_ref.at[place_of(at.chip_before(i))]).start()
+
+    loop(1, chips, pass_on)
+    loop(0, chips, lambda i: relay_copy(i, chunk_done).wait())
+    loop(1, chips, lambda i: chunk_copy(i).wait_send())
+    loop(1, planes, lambda i: plane_copy(i).wait_send())
+    loop(1, chips, lambda i: gather_copy(i).wait_send())
+
+
+def summed_image(field, basis, fib_size, pln_size):
+    chips = fib_size // 2
+    size = NX // 4 // 2 // chips
+    vmem = lambda *shape: pltpu.VMEM(shape, jnp.float32)
+    dma = lambda n: pltpu.SemaphoreType.DMA((n,))
+    image = pl.pallas_call(
+        functools.partial(reduce_kernel, fib_size, pln_size),
+        out_shape=jax.ShapeDtypeStruct((NX // 4, 4, RANK), jnp.float32),
+        in_specs=[pl.BlockSpec(memory_space=pltpu.VMEM)] * 2,
+        out_specs=pl.BlockSpec(memory_space=pltpu.VMEM),
+        scratch_shapes=[
+            vmem(NX // 4, 4, RANK), vmem(size * chips, 4, RANK), vmem(size * chips, 4, RANK),
+            vmem(chips, size, 4, RANK), vmem(size, 4, RANK), vmem(pln_size, size, 4, RANK),
+            vmem(size, 4, RANK),
+            dma(2), dma(chips), dma(chips), dma(pln_size), dma(pln_size), dma(chips), dma(chips),
+            dma(chips), dma(chips),
+        ],
+        compiler_params=pltpu.CompilerParams(collective_id=0, has_side_effects=True),
+    )(field, basis)
+    return image.reshape(NX, RANK)
 
 
 def per_device(nodal_values, interp_matrix, count_table, slot_order, start_basis):
@@ -89,8 +248,7 @@
     brick_grid = brick_values.reshape(owners, block_width, brick_values.shape[1] // 4)
     fibre_field = lax.all_to_all(brick_grid, "fib", split_axis=0, concat_axis=1, tiled=True)
     field = fibre_field[0]
-    coefficients = jnp.einsum("xf,xk->fk", field, start_basis, precision=HIGHEST)
-    image = lax.psum(jnp.dot(field, coefficients, precision=HIGHEST), ("fib", "pln"))
+    image = summed_image(field, start_basis, owners, lax.axis_size("pln"))
     normal = jnp.einsum("xk,xl->kl", image, image, precision=HIGHEST)
     right = jnp.einsum("xk,xf->kf", image, field, precision=HIGHEST)
     core_values = eliminate(normal, right)

time: 353 us -> 107 us (0.30)
  waiting for transfers between devices: 275 us -> 8.41 us
  Pallas kernels: 12.2 us -> 47.7 us
  between operations: 18.9 us -> 4.93 us
    psum x1 -> x0, waiting for transfers between devices: 267 us -> none  [per_device(): lax.psum(jnp.dot(field, coefficients, precision=HIGHEST), ('fib', 'pln'))]
    pallas_call x0 -> x1, Pallas kernels: none -> 35.4 us  [summed_image(): pl.pallas_call(functools.partial(reduce_kernel, fib_size, pln_size), out_...]
  transfers between devices with their start and end apart: 3 -> 2, of which waited for: 2 -> 1; matrix products, arithmetic and copies ran while one was open for 1% -> 2% of each run, Pallas kernels for 0% -> 0%
where the time goes in v2:
time: 107 us
  Pallas kernels  47.7 us (45%)
  blocking collectives  23.6 us (22%)
  matrix products  8.48 us (8%)
  waiting for transfers between devices  8.41 us (8%)
  starting transfers between devices  7.62 us (7%)
  local copies, waits for them, and re-layouts  5.09 us (5%)
  between operations  4.93 us (5%)
    pallas_call x1, Pallas kernels, summed_image(): pl.pallas_call(functools.partial(reduce_kernel, fib_size, pln_size), out_...  35.4 us
    all_to_all x1, blocking collectives, per_device(): lax.all_to_all(brick_grid, 'fib', split_axis=0, concat_axis=1, tiled=True)  23.6 us
    pallas_call x1, Pallas kernels, eliminate(): pl.pallas_call(eliminate_kernel, out_shape=jax.ShapeDtypeStruct((RANK, ri...  12.2 us
    ppermute x2, waiting for transfers between devices, shifted(): lax.ppermute(value, axis, [(i, (i + by) % peers) for i in range(peers)])  8.41 us
    ppermute x2, starting transfers between devices, shifted(): lax.ppermute(value, axis, [(i, (i + by) % peers) for i in range(peers)])  7.62 us
    dot_general x1, matrix products, per_device(): jnp.dot(node_rows, interp_matrix, precision=HIGHEST, preferred_element_ty...  3.4 us
    dot_general x1, matrix products, per_device(): right = jnp.einsum('xk,xf->kf', image, field, precision=HIGHEST)  2.54 us
    dot_general x1, matrix products, per_device(): normal = jnp.einsum('xk,xl->kl', image, image, precision=HIGHEST)  2.53 us
  transfers between devices with their start and end apart: 2, of which 1 were waited for; matrix products, arithmetic and copies ran while one was open for 2% of the time, Pallas kernels for 0%

profile of v2, /device:TPU:1, one launch (start us, length us, event | category | flops | bytes accessed | tf_op | source)
XLA Modules:
  0.0 106.5 jit_solution(4386824054967409533)
XLA Ops:
  0.0 0.0 copy-start
  0.0 0.8 copy.14
  0.8 0.6 constant_dynamic-slice_fusion.4
  4.3 0.0 copy-done
  4.3 0.0 copy-start.1
  4.3 0.0 copy-start.2
  4.4 3.4 %fusion = f32[288,512]{1,0:T(8,128)S(1)} fusion(f32[1000,512]{1,0:T(8,128)S(1)} %copy-done, f32[1,1,288,1000]{3,2,1,0:T(8,128)} %param.5), kind=kOutput, calls=%fused_computation.2 | convolution fusion | flops 1769472000 | bytes 3789824 | tf_op jit(solution)/shard_map/dot_general | solution.py:238
  7.8 0.1 fusion.5
  7.8 4.5 %collective-permute-start = (f32[96,512]{1,0:T(8,128)S(1)}, f32[96,512]{1,0:T(8,128)S(1)}, u32[]{:S(2)}, u32[]{:S(2)}) collective-permute-start(f32[96,512]{1,0:T(8,128)S(1)} %get-tuple-element.7), channel_id=1, source_target_pairs={{0,8},{8,16},{16,24},{24,32},{32,40},{40,48},{48,56},{56,64},{64,7... | collective-permute-start | bytes 589832 | tf_op jit(solution)/shard_map/ppermute | solution.py:17
  12.3 3.1 %collective-permute-start.1 = (f32[96,512]{1,0:T(8,128)S(1)}, f32[96,512]{1,0:T(8,128)S(1)}, u32[]{:S(2)}, u32[]{:S(2)}) collective-permute-start(f32[96,512]{1,0:T(8,128)S(1)} %get-tuple-element.6), channel_id=1, source_target_pairs={{0,16},{8,24},{16,32},{24,40},{32,48},{40,56},{48,64},{56,72},{64,... | collective-permute-start | bytes 589832 | tf_op jit(solution)/shard_map/ppermute | solution.py:17
  15.5 0.0 copy-done.1
  15.5 0.7 constant_dynamic-slice_fusion.2
  18.0 0.7 and_select_fusion.1
  18.7 0.0 copy-done.2
  18.7 1.2 %scatter_custom_fusion = s32[192]{0:T(256)S(1)} fusion(s32[192]{0:T(256)S(1)} %bitcast.23, s32[192]{0:T(256)S(1)} %and_select_fusion.1, s32[]{:T(128)} %constant.41.clone.1), kind=kCustom, calls=%fused_computation.21 | custom fusion | bytes 772 | tf_op jit(solution)/shard_map/scatter | solution.py:237
  20.0 0.0 collective-permute-done
  20.0 8.4 %collective-permute-done.1 = f32[96,512]{1,0:T(8,128)S(1)} collective-permute-done((f32[96,512]{1,0:T(8,128)S(1)}, f32[96,512]{1,0:T(8,128)S(1)}, u32[]{:S(2)}, u32[]{:S(2)}) %collective-permute-start.1) | collective-permute-done | bytes 196640 | tf_op jit(solution)/shard_map/ppermute | solution.py:17
  28.4 0.9 gather_fusion
  29.3 0.1 reshape.50
  29.4 23.6 %all_to_all.4 = f32[64,12,128]{2,1,0:T(8,128)S(1)} all-to-all(f32[64,12,128]{2,1,0:T(8,128)S(1)} %reshape.50), channel_id=1, replica_groups=mesh['fib'=64,'pln'=8] {'fib'}, dimensions={0} | all-to-all | bytes 786432 | tf_op jit(solution)/shard_map/all_to_all | solution.py:249
  53.0 0.8 squeeze.40.field_ref
  53.8 35.4 %shard_map.55 = f32[192,4,128]{2,1,0:T(4,128)} custom-call(f32[768,128]{1,0:T(8,128)} %squeeze.40.field_ref, f32[768,128]{1,0:T(8,128)} %basis_ref.1), custom_call_target="tpu_custom_call" | custom-call | tf_op jit(solution)/shard_map/pallas_call | solution.py:193
  89.2 2.5 %convolution_bitcast_fusion.normal_ref = f32[128,128]{1,0:T(8,128)} fusion(f32[192,4,128]{2,1,0:T(4,128)} %shard_map.55), kind=kOutput, calls=%fused_computation.4 | convolution fusion | flops 150994944 | bytes 458752 | tf_op jit(solution)/shard_map/xk,xl->kl/dot_general | solution.py:252
  91.8 2.5 %fusion.7.right_ref = f32[128,128]{1,0:T(8,128)} fusion(f32[768,128]{1,0:T(8,128)} %bitcast.21, f32[768,128]{1,0:T(8,128)} %squeeze.40.field_ref), kind=kOutput, calls=%fused_computation.25 | convolution fusion | flops 150994944 | bytes 851968 | tf_op jit(solution)/shard_map/xk,xf->kf/dot_general | solution.py:253
  94.3 12.2 %shard_map.56 = f32[128,128]{1,0:T(8,128)} custom-call(f32[128,128]{1,0:T(8,128)} %convolution_bitcast_fusion.normal_ref, f32[128,128]{1,0:T(8,128)} %fusion.7.right_ref), custom_call_target="tpu_custom_call" | custom-call | tf_op jit(solution)/shard_map/pallas_call | solution.py:43
  (5 shorter events, 0.1 us)
Async XLA Ops:
  0.0 4.3 %copy-start = (f32[1000,512]{1,0:T(8,128)S(1)}, f32[1000,512]{1,0:T(8,128)}, u32[]{:S(2)}) copy-start(f32[1000,512]{1,0:T(8,128)} %param.6) | copy-start | bytes 6144004
  4.3 11.1 %copy-start.1 = (s32[1,64,3]{1,0,2:T(1,128)S(1)}, s32[1,64,3]{1,0,2:T(1,128)}, u32[]{:S(2)}) copy-start(s32[1,64,3]{1,0,2:T(1,128)} %param.7) | copy-start | bytes 2308
  4.3 14.4 %copy-start.2 = (s32[1,1,192]{2,1,0:T(1,128)S(1)}, s32[1,1,192]{2,1,0:T(1,128)}, u32[]{:S(2)}) copy-start(s32[1,1,192]{2,1,0:T(1,128)} %param.8) | copy-start | bytes 2308
  7.8 12.1 %collective-permute-start = (f32[96,512]{1,0:T(8,128)S(1)}, f32[96,512]{1,0:T(8,128)S(1)}, u32[]{:S(2)}, u32[]{:S(2)}) collective-permute-start(f32[96,512]{1,0:T(8,128)S(1)} %get-tuple-element.7), channel_id=1, source_target_pairs={{0,8},{8,16},{16,24},{24,32},{32,40},{40,48},{48,56},{56,64},{64,7... | collective-permute-start | bytes 589832 | tf_op jit(solution)/shard_map/ppermute | solution.py:17
  12.3 16.1 %collective-permute-start.1 = (f32[96,512]{1,0:T(8,128)S(1)}, f32[96,512]{1,0:T(8,128)S(1)}, u32[]{:S(2)}, u32[]{:S(2)}) collective-permute-start(f32[96,512]{1,0:T(8,128)S(1)} %get-tuple-element.6), channel_id=1, source_target_pairs={{0,16},{8,24},{16,32},{24,40},{32,48},{40,56},{48,64},{56,72},{64,... | collective-permute-start | bytes 589832 | tf_op jit(solution)/shard_map/ppermute | solution.py:17

commit v3 on v2

--- a/solution.py
+++ b/solution.py
@@ -12,15 +12,24 @@
 HIGHEST = lax.Precision.HIGHEST
 
 
-def shifted(value, axis, by):
-    peers = lax.axis_size(axis)
-    return lax.ppermute(value, axis, [(i, (i + by) % peers) for i in range(peers)])
-
-
-def eliminate_kernel(normal_ref, right_ref, out_ref):
+WINDOW = 3
+CAP = 96
+R_ELEM = 192
+PIECES = NX // 4
+
+
+def eliminate_kernel(image_ref, field_ref, out_ref):
     blocks = RANK // 8
-    left = [normal_ref[8 * m:8 * m + 8, :] for m in range(blocks)]
-    right = [right_ref[8 * m:8 * m + 8, :] for m in range(blocks)]
+    image = image_ref[...]
+
+    def against_image(other):
+        return lax.dot_general(image, other, (((0,), (0,)), ((), ())), precision=HIGHEST,
+                               preferred_element_type=jnp.float32)
+
+    normal = against_image(image)
+    product = against_image(field_ref[...])
+    left = [normal[8 * m:8 * m + 8, :] for m in range(blocks)]
+    right = [product[8 * m:8 * m + 8, :] for m in range(blocks)]
     rows = lax.broadcasted_iota(jnp.int32, (8, RANK), 0)
     for k in range(RANK):
         i, r = divmod(k, 8)
@@ -39,13 +48,13 @@
             right[m] = right[m] - factor * scaled_right
 
 
-def eliminate(normal, right):
+def eliminate(image, field):
     return pl.pallas_call(
         eliminate_kernel,
-        out_shape=jax.ShapeDtypeStruct((RANK, right.shape[1]), jnp.float32),
+        out_shape=jax.ShapeDtypeStruct((RANK, field.shape[1]), jnp.float32),
         in_specs=[pl.BlockSpec(memory_space=pltpu.VMEM)] * 2,
         out_specs=pl.BlockSpec(memory_space=pltpu.VMEM),
-    )(normal, right)
+    )(image, field)
 
 
 MESH_ID = pl.DeviceIdType.MESH
@@ -77,6 +86,16 @@
         x = lax.rem(self.x + X_CHIPS - lax.rem(step, X_CHIPS), X_CHIPS)
         return z * X_CHIPS + x
 
+    def along(self, step):
+        core = lax.rem(self.core + lax.rem(step, 2), 2)
+        return self.chip_at(lax.div(step, 2)) * 2 + core
+
+    def after(self, distance):
+        return lax.rem(self.fib + distance, 2 * self.chips)
+
+    def in_fib(self, fib):
+        return {"fib": fib, "pln": self.pln}
+
     def on_chip(self, chip):
         return {"fib": chip * 2 + self.core, "pln": self.pln}
 
@@ -98,30 +117,98 @@
     lax.fori_loop(low, high, step, 0)
 
 
-def reduce_kernel(fib_size, pln_size, field_ref, basis_ref, image_ref, part, other, half, chip_parts,
-                  chunk_sum, plane_parts, chunk_done, core_sems, chip_send, chip_recv, plane_send,
-                  plane_recv, gather_send, gather_recv, relay_send, relay_recv):
+def pair(value):
+    high = value.astype(jnp.bfloat16)
+    return high, (value - high.astype(jnp.float32)).astype(jnp.bfloat16)
+
+
+def mult(left, right):
+    return jnp.dot(left, right, preferred_element_type=jnp.float32)
+
+
+def step_kernel(fib_size, pln_size, nodes_ref, interp_ref, table_ref, order_ref, basis_ref, field_ref, image_ref,
+                outgoing, incoming, brick, part, other, half, chip_parts, chunk_sum, plane_parts, chunk_done,
+                shift_send, shift_recv, tile_send, tile_recv, core_sems, chip_send, chip_recv, plane_send,
+                plane_recv, gather_send, gather_recv, relay_send, relay_recv):
     at = Place(fib_size, pln_size)
     chips, planes = at.chips, at.planes
-    size = NX // 4 // 2 // chips
+    size = PIECES // 2 // chips
     split = size * chips
+    run = PIECES // fib_size
     barrier = pltpu.get_barrier_semaphore()
 
     def greet(device):
         pl.semaphore_signal(barrier, inc=1, device_id=device, device_id_type=MESH_ID)
 
-    greet(at.other_core())
-    loop(1, chips, lambda i: greet(at.on_chip(at.chip_at(i))))
+    loop(1, fib_size, lambda i: greet(at.in_fib(at.along(i))))
     loop(1, planes, lambda i: greet(at.in_plane(i)))
 
-    field = field_ref[...]
+    starts = [0]
+    for distance in range(WINDOW - 1):
+        starts.append(starts[-1] + table_ref[at.after(distance), distance])
+    interp_high, interp_low = pair(interp_ref[...])
+    nodes_high, nodes_low = pair(nodes_ref[...])
+    slots = (lax.broadcasted_iota(jnp.int32, (CAP, WINDOW * CAP), 1)
+             - lax.broadcasted_iota(jnp.int32, (CAP, WINDOW * CAP), 0))
+
+    def shift_copy(distance):
+        return remote(outgoing.at[distance - 1], incoming.at[distance], shift_send.at[distance - 1],
+                      shift_recv.at[distance - 1], at.in_fib(at.after(distance)))
+
+    for distance in range(WINDOW - 1, -1, -1):
+        if distance == 0:
+            high, low = nodes_high[:CAP], nodes_low[:CAP]
+        else:
+            window = jnp.where(slots == starts[distance], 1.0, 0.0).astype(jnp.bfloat16)
+            high = mult(window, nodes_high).astype(jnp.bfloat16)
+            low = mult(window, nodes_low).astype(jnp.bfloat16)
+        values = mult(high, interp_high) + (mult(high, interp_low) + mult(low, interp_high))
+        if distance == 0:
+            incoming[0] = values
+        else:
+            outgoing[distance - 1] = values
+            if distance == WINDOW - 1:
+                pl.semaphore_wait(barrier, fib_size + planes - 2)
+            shift_copy(distance).start()
+
+    taken_near = table_ref[at.fib, 1]
+    taken_far = table_ref[at.fib, 2]
+    ranks = lax.broadcasted_iota(jnp.int32, (1, R_ELEM), 1)
+    source = jnp.where(ranks < taken_far, 2 * CAP + ranks,
+                       jnp.where(ranks < taken_far + taken_near, CAP + ranks - taken_far,
+                                 ranks - taken_far - taken_near))
+    places = lax.broadcasted_iota(jnp.int32, (R_ELEM, R_ELEM), 0)
+    chosen = jnp.where(order_ref[...] == places, source.astype(jnp.float32), 0.0)
+    chosen = jnp.sum(chosen, axis=1, keepdims=True).astype(jnp.int32)
+    select = lax.broadcasted_iota(jnp.int32, (R_ELEM, WINDOW * CAP), 1) == chosen
+    select = jnp.where(select, 1.0, 0.0).astype(jnp.bfloat16)
+    for distance in range(1, WINDOW):
+        shift_copy(distance).wait_recv()
+    rows = incoming[...].reshape(WINDOW * CAP, 4 * RANK)
+    high, low = pair(rows)
+    rest = (rows - high.astype(jnp.float32)) - low.astype(jnp.float32)
+    values = mult(select, high) + (mult(select, low) + mult(select, rest.astype(jnp.bfloat16)))
+    for l in range(4):
+        brick[:, l, :] = values[:, l * RANK:(l + 1) * RANK]
+
+    def own_pieces(fib):
+        return pl.ds(fib * run, run)
+
+    def tile_copy(i):
+        peer = at.along(i)
+        return remote(brick.at[own_pieces(peer)], field_ref.at[own_pieces(at.fib)], tile_send.at[i],
+                      tile_recv.at[i], at.in_fib(peer))
+
+    loop(1, fib_size, lambda i: tile_copy(i).start())
+    field_ref[own_pieces(at.fib)] = brick[own_pieces(at.fib)]
+    loop(1, fib_size, lambda i: tile_copy(i).wait_recv())
+
+    field = field_ref[...].reshape(NX, RANK)
     coefficients = lax.dot_general(
         field, basis_ref[...], (((0,), (0,)), ((), ())), precision=HIGHEST,
         preferred_element_type=jnp.float32)
     product = jnp.dot(field, coefficients, precision=HIGHEST, preferred_element_type=jnp.float32)
-    part[...] = product.reshape(NX // 4, 4, RANK)
-
-    pl.semaphore_wait(barrier, chips + planes - 1)
+    part[...] = product.reshape(PIECES, 4, RANK)
 
     swap = remote(part.at[pl.ds((1 - at.core) * split, split)], other, core_sems.at[0], core_sems.at[1],
                   at.other_core())
@@ -183,76 +270,42 @@
     loop(1, chips, lambda i: chunk_copy(i).wait_send())
     loop(1, planes, lambda i: plane_copy(i).wait_send())
     loop(1, chips, lambda i: gather_copy(i).wait_send())
-
-
-def summed_image(field, basis, fib_size, pln_size):
+    loop(1, fib_size, lambda i: tile_copy(i).wait_send())
+    for distance in range(1, WINDOW):
+        shift_copy(distance).wait_send()
+
+
+def field_and_image(nodes, interp, table, order, basis, fib_size, pln_size):
     chips = fib_size // 2
-    size = NX // 4 // 2 // chips
+    size = PIECES // 2 // chips
     vmem = lambda *shape: pltpu.VMEM(shape, jnp.float32)
     dma = lambda n: pltpu.SemaphoreType.DMA((n,))
-    image = pl.pallas_call(
-        functools.partial(reduce_kernel, fib_size, pln_size),
-        out_shape=jax.ShapeDtypeStruct((NX // 4, 4, RANK), jnp.float32),
-        in_specs=[pl.BlockSpec(memory_space=pltpu.VMEM)] * 2,
-        out_specs=pl.BlockSpec(memory_space=pltpu.VMEM),
+    whole = pl.BlockSpec(memory_space=pltpu.VMEM)
+    pieces = jax.ShapeDtypeStruct((PIECES, 4, RANK), jnp.float32)
+    field, image = pl.pallas_call(
+        functools.partial(step_kernel, fib_size, pln_size),
+        out_shape=(pieces, pieces),
+        in_specs=[whole, whole, pl.BlockSpec(memory_space=pltpu.SMEM), whole, whole],
+        out_specs=(whole, whole),
         scratch_shapes=[
-            vmem(NX // 4, 4, RANK), vmem(size * chips, 4, RANK), vmem(size * chips, 4, RANK),
+            vmem(WINDOW - 1, CAP, 4 * RANK), vmem(WINDOW, CAP, 4 * RANK), vmem(PIECES, 4, RANK),
+            vmem(PIECES, 4, RANK), vmem(size * chips, 4, RANK), vmem(size * chips, 4, RANK),
             vmem(chips, size, 4, RANK), vmem(size, 4, RANK), vmem(pln_size, size, 4, RANK),
             vmem(size, 4, RANK),
+            dma(WINDOW - 1), dma(WINDOW - 1), dma(fib_size), dma(fib_size),
             dma(2), dma(chips), dma(chips), dma(pln_size), dma(pln_size), dma(chips), dma(chips),
             dma(chips), dma(chips),
         ],
         compiler_params=pltpu.CompilerParams(collective_id=0, has_side_effects=True),
-    )(field, basis)
-    return image.reshape(NX, RANK)
+    )(nodes, interp, table, order, basis)
+    return field.reshape(NX, RANK), image.reshape(NX, RANK)
 
 
 def per_device(nodal_values, interp_matrix, count_table, slot_order, start_basis):
-    node_rows = nodal_values[0, 0]
-    owner_table = count_table[0]
-    brick_order = slot_order[0, 0]
-    owners = lax.axis_size("fib")
-    own_index = lax.axis_index("fib")
-    window = owner_table.shape[1]
-    capacity = node_rows.shape[0] // window
-    elements = brick_order.shape[0]
-    block_width = NX // owners
-    send_start = []
-    running = jnp.int32(0)
-    for distance in range(window):
-        send_start.append(running)
-        column = owner_table[:, distance]
-        running = running + lax.dynamic_index_in_dim(
-            column, (own_index + distance) % owners, 0, keepdims=False
-        )
-    own_counts = lax.dynamic_index_in_dim(owner_table, own_index, 0, keepdims=False)
-    positions = jnp.arange(elements, dtype=jnp.int32)
-    combined_index = jnp.zeros((elements,), jnp.int32)
-    offset = jnp.int32(0)
-    for distance in range(window - 1, -1, -1):
-        taken_count = own_counts[distance]
-        inside = (positions >= offset) & (positions < offset + taken_count)
-        combined_index = jnp.where(inside, distance * capacity + positions - offset, combined_index)
-        offset = offset + taken_count
-    brick_source = jnp.zeros((elements,), jnp.int32).at[brick_order].set(combined_index)
-    grid_rows = jnp.dot(
-        node_rows, interp_matrix, precision=HIGHEST, preferred_element_type=jnp.float32
-    )
-    received = []
-    for distance in range(window):
-        send_piece = lax.dynamic_slice_in_dim(grid_rows, send_start[distance], capacity, 0)
-        if distance > 0:
-            send_piece = shifted(send_piece, "fib", distance)
-        received.append(send_piece)
-    brick_values = jnp.concatenate(received, axis=0)[brick_source]
-    brick_grid = brick_values.reshape(owners, block_width, brick_values.shape[1] // 4)
-    fibre_field = lax.all_to_all(brick_grid, "fib", split_axis=0, concat_axis=1, tiled=True)
-    field = fibre_field[0]
-    image = summed_image(field, start_basis, owners, lax.axis_size("pln"))
-    normal = jnp.einsum("xk,xl->kl", image, image, precision=HIGHEST)
-    right = jnp.einsum("xk,xf->kf", image, field, precision=HIGHEST)
-    core_values = eliminate(normal, right)
-    return core_values[None, None]
+    field, image = field_and_image(
+        nodal_values[0, 0], interp_matrix, count_table[0], slot_order[0], start_basis,
+        lax.axis_size("fib"), lax.axis_size("pln"))
+    return eliminate(image, field)[None, None]
 
 
 def solution(mesh):

time: 107 us -> 85.5 us (0.80)
  Pallas kernels: 47.7 us -> 83.9 us
  blocking collectives: 23.6 us -> 0 us
  matrix products: 8.48 us -> 0 us
  waiting for transfers between devices: 8.41 us -> 0 us
  starting transfers between devices: 7.62 us -> 0 us
  between operations: 4.93 us -> 0.01 us
  local copies, waits for them, and re-layouts: 5.09 us -> 1.38 us
    pallas_call x2, Pallas kernels: 47.7 us -> 83.9 us  [the longest x1 71 us: field_and_image(): pl.pallas_call(functools.partial(step_kernel, fib_size, pln_size), out_sh...]
    all_to_all x1 -> x0, blocking collectives: 23.6 us -> none  [per_device(): lax.all_to_all(brick_grid, 'fib', split_axis=0, concat_axis=1, tiled=True)]
    dot_general x3 -> x0, matrix products: 8.48 us -> none  [the longest x1 3.4 us: per_device(): jnp.dot(node_rows, interp_matrix, precision=HIGHEST, preferred_element_ty...]
    ppermute x2 -> x0, waiting for transfers between devices: 8.41 us -> none  [shifted(): lax.ppermute(value, axis, [(i, (i + by) % peers) for i in range(peers)])]
    ppermute x2 -> x0, starting transfers between devices: 7.62 us -> none  [shifted(): lax.ppermute(value, axis, [(i, (i + by) % peers) for i in range(peers)])]
    scatter x1 -> x0, local copies, waits for them, and re-layouts: 1.2 us -> none  [per_device(): jnp.zeros((elements,), jnp.int32).at[brick_order].set(combined_index)]
  transfers between devices with their start and end apart: 2 -> 0, of which waited for: 1 -> 0; matrix products, arithmetic and copies ran while one was open for 2% -> 0% of each run, Pallas kernels for 0% -> 0%
where the time goes in v3:
time: 85.5 us; the launch traced here: 85.3 us
  Pallas kernels  83.9 us (98%)
  local copies, waits for them, and re-layouts  1.38 us (2%)
    pallas_call x1, Pallas kernels, field_and_image(): pl.pallas_call(functools.partial(step_kernel, fib_size, pln_size), out_sh...  71 us
    pallas_call x1, Pallas kernels, eliminate(): pl.pallas_call(eliminate_kernel, out_shape=jax.ShapeDtypeStruct((RANK, fi...  13 us

profile of v3, /device:TPU:1, one launch (start us, length us, event | category | flops | bytes accessed | tf_op | source)
XLA Modules:
  0.0 85.3 jit_solution(17662676602057809047)
XLA Ops:
  0.0 1.4 %copy.6 = s32[1,64,3]{2,1,0:T(8,128)} copy(s32[1,64,3]{1,0,2:T(1,128)} %param.7) | data formatting | bytes 1536 | tf_op args[2]
  1.4 71.0 %shard_map.55 = (f32[192,4,128]{2,1,0:T(4,128)}, f32[192,4,128]{2,1,0:T(4,128)}) custom-call(f32[288,1000]{1,0:T(8,128)} %bitcast.6, f32[1000,512]{1,0:T(8,128)} %interp_ref.1, s32[64,3]{1,0:T(8,128)} %bitcast.9, s32[1,192]{1,0:T(1,128)} %bitcast.10, f32[768,128]{1,0:T(8,128)} %basis_ref.1), custom_call_target="tpu_custom_call" | custom-call | tf_op jit(solution)/shard_map/pallas_call | solution.py:285
  72.3 13.0 %shard_map.56 = f32[128,128]{1,0:T(8,128)} custom-call(f32[768,128]{1,0:T(8,128)} %bitcast.8, f32[768,128]{1,0:T(8,128)} %bitcast.7), custom_call_target="tpu_custom_call" | custom-call | tf_op jit(solution)/shard_map/pallas_call | solution.py:52

commit v4 on v3

v4 whole, which is shorter than its diff:
```python
import functools

import jax
import jax.numpy as jnp
from jax import lax
from jax.experimental import pallas as pl
from jax.experimental.pallas import tpu as pltpu
from jax.sharding import PartitionSpec as P

NX = 768
RANK = 128
WINDOW = 3
CAP = 96
R_ELEM = 192
PIECES = NX // 4
X_CHIPS = 4
CUTS = 4
PIVOTS = 4
HIGHEST = lax.Precision.HIGHEST
MESH_ID = pl.DeviceIdType.MESH


def eliminate_kernel(system_ref, out_ref):
    blocks = RANK // 8
    left = [system_ref[8 * m:8 * m + 8, :RANK] for m in range(blocks)]
    right = [system_ref[8 * m:8 * m + 8, RANK:] for m in range(blocks)]
    rows = lax.broadcasted_iota(jnp.int32, (8, RANK), 0)

    def spread(row):
        return jnp.broadcast_to(row, (8, RANK))

    for k in range(0, RANK, PIVOTS):
        i, r = divmod(k, 8)
        row_left = [spread(left[i][r + a:r + a + 1, :]) for a in range(PIVOTS)]
        row_right = [spread(right[i][r + a:r + a + 1, :]) for a in range(PIVOTS)]
        corner = [[spread(row_left[a][:, k + b:k + b + 1]) if b >= a else None for b in range(PIVOTS)]
                  for a in range(PIVOTS)]
        ratio = [[None] * PIVOTS for _ in range(PIVOTS)]
        inverse = []
        for a in range(PIVOTS):
            inverse.append(1.0 / corner[a][a])
            for b in range(a + 1, PIVOTS):
                ratio[a][b] = corner[a][b] * inverse[a]
                for c in range(b, PIVOTS):
                    corner[b][c] = corner[b][c] - ratio[a][b] * corner[a][c]
                row_left[b] = row_left[b] - ratio[a][b] * row_left[a]
                row_right[b] = row_right[b] - ratio[a][b] * row_right[a]
        for a in range(PIVOTS):
            out_ref[k + a:k + a + 1, :] = (row_right[a] * lax.rsqrt(corner[a][a]))[:1]
        scaled_left = [row_left[a] * inverse[a] for a in range(PIVOTS)]
        scaled_right = [row_right[a] * inverse[a] for a in range(PIVOTS)]
        for m in range(i if r + PIVOTS < 8 else i + 1, blocks):
            factor = []
            for a in range(PIVOTS):
                column = spread(left[m][:, k + a:k + a + 1])
                if m == i:
                    column = jnp.where(rows >= r + PIVOTS, column, 0.0)
                for b in range(a):
                    column = column - ratio[b][a] * factor[b]
                factor.append(column)
            for a in range(PIVOTS):
                left[m] = left[m] - factor[a] * scaled_left[a]
                right[m] = right[m] - factor[a] * scaled_right[a]


def eliminate(system):
    return pl.pallas_call(
        eliminate_kernel,
        out_shape=jax.ShapeDtypeStruct((RANK, system.shape[1] - RANK), jnp.float32),
        in_specs=[pl.BlockSpec(memory_space=pltpu.VMEM)],
        out_specs=pl.BlockSpec(memory_space=pltpu.VMEM),
    )(system)


def remote(src, dst, send_sem, recv_sem, device):
    return pltpu.make_async_remote_copy(
        src_ref=src, dst_ref=dst, send_sem=send_sem, recv_sem=recv_sem,
        device_id=device, device_id_type=MESH_ID,
    )


def loop(low, high, body):
    def step(i, carry):
        body(i)
        return carry
    lax.fori_loop(low, high, step, 0)


class Place:
    def __init__(self, fib_size, pln_size):
        self.fib_size = fib_size
        self.chips = fib_size // 2
        self.depth = self.chips // X_CHIPS
        self.planes = pln_size
        self.fib = lax.axis_index("fib")
        self.pln = lax.axis_index("pln")
        self.core = lax.rem(self.fib, 2)
        self.chip = lax.div(self.fib, 2)
        self.z = lax.div(self.chip, X_CHIPS)
        self.x = lax.rem(self.chip, X_CHIPS)
        self.x_after = [lax.rem(self.x + step, X_CHIPS) for step in range(X_CHIPS)]
        self.x_before = [lax.rem(self.x + X_CHIPS - step, X_CHIPS) for step in range(X_CHIPS)]

    def at_fib(self, fib):
        return {"fib": fib, "pln": self.pln}

    def on_chip(self, chip):
        return self.at_fib(chip * 2 + self.core)

    def other_core(self):
        return self.at_fib(self.chip * 2 + 1 - self.core)

    def after(self, distance):
        return lax.rem(self.fib + distance, self.fib_size)

    def in_plane(self, step):
        return {"fib": self.fib, "pln": lax.rem(self.pln + step, self.planes)}

    def over_depth(self, row, far_first):
        if far_first:
            skip = (self.depth // 2 - 2) % (self.depth - 1)
            loop(0, self.depth - 1, lambda n: row(lax.rem(n + skip, self.depth - 1) + 1, True))
            row(0, False)
        else:
            row(0, False)
            loop(1, self.depth, lambda n: row(n, True))

    def each_chip(self, body, far_first=False):
        def row(z_step, with_own):
            ahead = lax.rem(self.z + z_step, self.depth) * X_CHIPS
            behind = lax.rem(self.z + self.depth - z_step, self.depth) * X_CHIPS
            for x_step in range(0 if with_own else 1, X_CHIPS):
                body(z_step * X_CHIPS + x_step, ahead + self.x_after[x_step], behind + self.x_before[x_step])
        self.over_depth(row, far_first)

    def each_device(self, body, far_first=False):
        def row(z_step, with_own):
            ahead = lax.rem(self.z + z_step, self.depth) * X_CHIPS
            for x_step in range(X_CHIPS):
                for turn in range(2):
                    if with_own or x_step or turn:
                        core = self.core if turn == 0 else 1 - self.core
                        body((z_step * X_CHIPS + x_step) * 2 + turn, (ahead + self.x_after[x_step]) * 2 + core)
        self.over_depth(row, far_first)


def pair(value):
    high = value.astype(jnp.bfloat16)
    return high, (value - high.astype(jnp.float32)).astype(jnp.bfloat16)


def mult(left, right):
    return jnp.dot(left, right, preferred_element_type=jnp.float32)


def gram(left, right):
    return lax.dot_general(left, right, (((0,), (0,)), ((), ())), precision=HIGHEST,
                           preferred_element_type=jnp.float32)


def step_kernel(fib_size, pln_size, nodes_hbm, interp_hbm, table_ref, order_ref, basis_hbm, system_ref,
                nodes_ref, interp_ref, basis_ref, outgoing, incoming, brick, field_ref, image_ref, part, other,
                half, chip_parts, chunk_sum, plane_parts, chunk_done, load_sems, shift_send, shift_recv,
                tile_send, tile_recv, core_sems, chip_send, chip_recv, plane_send, plane_recv, gather_send,
                gather_recv, relay_send, relay_recv):
    at = Place(fib_size, pln_size)
    chips, planes = at.chips, at.planes
    size = PIECES // 2 // chips
    split = size * chips
    run = PIECES // fib_size
    barrier = pltpu.get_barrier_semaphore()
    loads = [pltpu.make_async_copy(nodes_hbm, nodes_ref, load_sems.at[0]),
             pltpu.make_async_copy(interp_hbm, interp_ref, load_sems.at[1]),
             pltpu.make_async_copy(basis_hbm, basis_ref, load_sems.at[2])]
    for load in loads:
        load.start()

    def greet(device):
        pl.semaphore_signal(barrier, inc=1, device_id=device, device_id_type=MESH_ID)

    at.each_device(lambda i, fib: greet(at.at_fib(fib)), far_first=True)
    loop(1, planes, lambda i: greet(at.in_plane(i)))

    starts = [0]
    for distance in range(WINDOW - 1):
        starts.append(starts[-1] + table_ref[distance, 0, at.after(distance)])
    slots = (lax.broadcasted_iota(jnp.int32, (CAP, WINDOW * CAP), 1)
             - lax.broadcasted_iota(jnp.int32, (CAP, WINDOW * CAP), 0))
    for load in loads:
        load.wait()
    interp_high, interp_low = pair(interp_ref[...])
    nodes_high, nodes_low = pair(nodes_ref[...])

    def shift_copies(distance):
        rows = CAP // CUTS
        return [remote(outgoing.at[distance - 1, pl.ds(cut * rows, rows)],
                       incoming.at[distance, pl.ds(cut * rows, rows)],
                       shift_send.at[distance - 1, cut], shift_recv.at[distance - 1, cut],
                       at.at_fib(at.after(distance))) for cut in range(CUTS)]

    for distance in range(WINDOW - 1, -1, -1):
        if distance == 0:
            high, low = nodes_high[:CAP], nodes_low[:CAP]
        else:
            window = jnp.where(slots == starts[distance], 1.0, 0.0).astype(jnp.bfloat16)
            high = mult(window, nodes_high).astype(jnp.bfloat16)
            low = mult(window, nodes_low).astype(jnp.bfloat16)
        values = mult(high, interp_high) + (mult(high, interp_low) + mult(low, interp_high))
        if distance == 0:
            incoming[0] = values
        else:
            outgoing[distance - 1] = values
            if distance == WINDOW - 1:
                pl.semaphore_wait(barrier, fib_size + planes - 2)
            for copy in shift_copies(distance):
                copy.start()

    taken_near = table_ref[1, 0, at.fib]
    taken_far = table_ref[2, 0, at.fib]
    ranks = lax.broadcasted_iota(jnp.int32, (1, R_ELEM), 1)
    source = jnp.where(ranks < taken_far, 2 * CAP + ranks,
                       jnp.where(ranks < taken_far + taken_near, CAP + ranks - taken_far,
                                 ranks - taken_far - taken_near))
    places = lax.broadcasted_iota(jnp.int32, (R_ELEM, R_ELEM), 0)
    chosen = jnp.where(order_ref[...] == places, source.astype(jnp.float32), 0.0)
    chosen = jnp.sum(chosen, axis=1, keepdims=True).astype(jnp.int32)
    select = lax.broadcasted_iota(jnp.int32, (R_ELEM, WINDOW * CAP), 1) == chosen
    select = jnp.where(select, 1.0, 0.0).astype(jnp.bfloat16)
    for distance in range(WINDOW - 1, 0, -1):
        for copy in shift_copies(distance):
            copy.wait_recv()
    rows = incoming[...].reshape(WINDOW * CAP, 4 * RANK)
    high, low = pair(rows)
    rest = (rows - high.astype(jnp.float32)) - low.astype(jnp.float32)
    values = mult(select, high) + (mult(select, low) + mult(select, rest.astype(jnp.bfloat16)))
    for l in range(4):
        brick[:, l, :] = values[:, l * RANK:(l + 1) * RANK]

    def own_pieces(fib):
        return pl.ds(fib * run, run)

    def tile_copy(i, peer):
        return remote(brick.at[own_pieces(peer)], field_ref.at[own_pieces(at.fib)], tile_send.at[i],
                      tile_recv.at[i], at.at_fib(peer))

    at.each_device(lambda i, peer: tile_copy(i, peer).start(), far_first=True)
    field_ref[own_pieces(at.fib)] = brick[own_pieces(at.fib)]
    loop(1, fib_size, lambda i: tile_copy(i, at.fib).wait_recv())

    field = field_ref[...].reshape(NX, RANK)
    product = jnp.dot(field, gram(field, basis_ref[...]), precision=HIGHEST,
                      preferred_element_type=jnp.float32)
    part[...] = product.reshape(PIECES, 4, RANK)

    swap = remote(part.at[pl.ds((1 - at.core) * split, split)], other, core_sems.at[0], core_sems.at[1],
                  at.other_core())
    swap.start()
    swap.wait()
    half[...] = part[pl.ds(at.core * split, split)] + other[...]

    def chunk_copy(i, chip):
        return remote(half.at[pl.ds(chip * size, size)], chip_parts.at[i], chip_send.at[i], chip_recv.at[i],
                      at.on_chip(chip))

    at.each_chip(lambda i, chip, back: chunk_copy(i, chip).start(), far_first=True)
    chunk_sum[...] = half[pl.ds(at.chip * size, size)]

    def add_chunk(i):
        chunk_copy(i, at.chip).wait_recv()
        chunk_sum[...] += chip_parts[i]

    loop(1, chips, add_chunk)

    def plane_copy(i):
        return remote(chunk_sum, plane_parts.at[i], plane_send.at[i], plane_recv.at[i], at.in_plane(i))

    loop(1, planes, lambda i: plane_copy(i).start())
    chunk_done[...] = chunk_sum[...]

    def add_plane(i):
        plane_copy(i).wait_recv()
        chunk_done[...] += plane_parts[i]

    loop(1, planes, add_plane)

    def place_of(chip):
        return pl.ds(at.core * split + chip * size, size)

    def gather_copy(i, chip):
        return remote(chunk_done, image_ref.at[place_of(at.chip)], gather_send.at[i], gather_recv.at[i],
                      at.on_chip(chip))

    def relay_copy(i, source, chip):
        return remote(source, image_ref.at[place_of(chip)], relay_send.at[i], relay_recv.at[i], at.other_core())

    at.each_chip(lambda i, chip, back: gather_copy(i, chip).start(), far_first=True)
    relay_copy(0, chunk_done, at.chip).start()
    image_ref[place_of(at.chip)] = chunk_done[...]

    def pass_on(i, chip, back):
        gather_copy(i, chip).wait_recv()
        relay_copy(i, image_ref.at[place_of(back)], back).start()

    at.each_chip(pass_on)
    loop(0, chips, lambda i: relay_copy(i, chunk_done, at.chip).wait())

    image = image_ref[...].reshape(NX, RANK)
    system_ref[:, :RANK] = gram(image, image)
    system_ref[:, RANK:] = gram(image, field_ref[...].reshape(NX, RANK))

    loop(1, fib_size, lambda i: tile_copy(i, at.fib).wait_send())
    loop(1, chips, lambda i: chunk_copy(i, at.chip).wait_send())
    loop(1, planes, lambda i: plane_copy(i).wait_send())
    loop(1, chips, lambda i: gather_copy(i, at.chip).wait_send())
    for distance in range(1, WINDOW):
        for copy in shift_copies(distance):
            copy.wait_send()


def normal_system(nodes, interp, table, order, basis, fib_size, pln_size):
    chips = fib_size // 2
    size = PIECES // 2 // chips
    vmem = lambda *shape: pltpu.VMEM(shape, jnp.float32)
    dma = lambda *n: pltpu.SemaphoreType.DMA(n)
    whole = pl.BlockSpec(memory_space=pltpu.VMEM)
    away = pl.BlockSpec(memory_space=pl.ANY)
    return pl.pallas_call(
        functools.partial(step_kernel, fib_size, pln_size),
        out_shape=jax.ShapeDtypeStruct((RANK, 2 * RANK), jnp.float32),
        in_specs=[away, away, pl.BlockSpec(memory_space=pltpu.SMEM), whole, away],
        out_specs=whole,
        scratch_shapes=[
            vmem(*nodes.shape), vmem(*interp.shape), vmem(*basis.shape),
            vmem(WINDOW - 1, CAP, 4 * RANK), vmem(WINDOW, CAP, 4 * RANK), vmem(PIECES, 4, RANK),
            vmem(PIECES, 4, RANK), vmem(PIECES, 4, RANK),
            vmem(PIECES, 4, RANK), vmem(size * chips, 4, RANK), vmem(size * chips, 4, RANK),
            vmem(chips, size, 4, RANK), vmem(size, 4, RANK), vmem(pln_size, size, 4, RANK),
            vmem(size, 4, RANK),
            dma(3), dma(WINDOW - 1, CUTS), dma(WINDOW - 1, CUTS), dma(fib_size), dma(fib_size),
            dma(2), dma(chips), dma(chips), dma(pln_size), dma(pln_size), dma(chips), dma(chips),
            dma(chips), dma(chips),
        ],
        compiler_params=pltpu.CompilerParams(collective_id=0, has_side_effects=True),
    )(nodes, interp, table, order, basis)


def per_device(nodal_values, interp_matrix, count_table, slot_order, start_basis):
    system = normal_system(
        nodal_values[0, 0], interp_matrix, jnp.transpose(count_table, (2, 0, 1)), slot_order[0], start_basis,
        lax.axis_size("fib"), lax.axis_size("pln"))
    return eliminate(system)[None, None]


def solution(mesh):
    placed = (P("pln", "fib", None, None), P(), P("pln", None, None), P("pln", "fib", None), P())
    return jax.shard_map(
        per_device,
        mesh=mesh,
        in_specs=placed,
        out_specs=P("pln", "fib", None, None),
        check_vma=False,
    )
```

time: 85.5 us -> 74.7 us (0.87)
  Pallas kernels: 83.9 us -> 74.6 us
  local copies, waits for them, and re-layouts: 1.38 us -> 0 us
    pallas_call x2, Pallas kernels: 83.9 us -> 74.6 us  [the longest x1 67.2 us: normal_system(): pl.pallas_call(functools.partial(step_kernel, fib_size, pln_size), out_sh...]
    unnamed x1 -> x0, local copies, waits for them, and re-layouts: 1.38 us -> none
where the time goes in v4:
time: 74.7 us; the launch traced here: 74.6 us
  Pallas kernels  74.6 us (100%)
    pallas_call x1, Pallas kernels, normal_system(): pl.pallas_call(functools.partial(step_kernel, fib_size, pln_size), out_sh...  67.2 us
    pallas_call x1, Pallas kernels, eliminate(): pl.pallas_call(eliminate_kernel, out_shape=jax.ShapeDtypeStruct((RANK, sy...  7.35 us

profile of v4, /device:TPU:1, one launch (start us, length us, event | category | flops | bytes accessed | tf_op | source)
XLA Modules:
  0.0 74.6 jit_solution(2545973065048243517)
XLA Ops:
  0.0 67.2 %shard_map.55.system_ref = f32[128,256]{1,0:T(8,128)} custom-call(f32[288,1000]{1,0:T(8,128)} %bitcast.4, f32[1000,512]{1,0:T(8,128)} %interp_hbm.1, s32[3,1,64]{2,1,0:T(1,128)} %bitcast.5, s32[1,192]{1,0:T(1,128)} %bitcast.6, f32[768,128]{1,0:T(8,128)} %basis_hbm.1), custom_call_target="tpu_custom_call" | custom-call | tf_op jit(solution)/shard_map/pallas_call | solution.py:327
  67.2 7.4 %shard_map.56 = f32[128,128]{1,0:T(8,128)} custom-call(f32[128,256]{1,0:T(8,128)} %shard_map.55.system_ref), custom_call_target="tpu_custom_call" | custom-call | tf_op jit(solution)/shard_map/pallas_call | solution.py:67

commit v5 on v4

--- a/solution.py
+++ b/solution.py
@@ -15,7 +15,7 @@
 PIECES = NX // 4
 X_CHIPS = 4
 CUTS = 4
-PIVOTS = 4
+PIVOTS = 8
 HIGHEST = lax.Precision.HIGHEST
 MESH_ID = pl.DeviceIdType.MESH
 
@@ -172,14 +172,14 @@
     loads = [pltpu.make_async_copy(nodes_hbm, nodes_ref, load_sems.at[0]),
              pltpu.make_async_copy(interp_hbm, interp_ref, load_sems.at[1]),
              pltpu.make_async_copy(basis_hbm, basis_ref, load_sems.at[2])]
+
+    def greet(device):
+        pl.semaphore_signal(barrier, inc=1, device_id=device, device_id_type=MESH_ID)
+
+    at.each_device(lambda i, fib: greet(at.at_fib(fib)), far_first=True)
+    loop(1, planes, lambda i: greet(at.in_plane(i)))
     for load in loads:
         load.start()
-
-    def greet(device):
-        pl.semaphore_signal(barrier, inc=1, device_id=device, device_id_type=MESH_ID)
-
-    at.each_device(lambda i, fib: greet(at.at_fib(fib)), far_first=True)
-    loop(1, planes, lambda i: greet(at.in_plane(i)))
 
     starts = [0]
     for distance in range(WINDOW - 1):

time: 74.7 us -> 72.9 us (0.976)
  Pallas kernels: 74.6 us -> 72.8 us
    pallas_call x1, Pallas kernels: 7.35 us -> 5.54 us  [eliminate(): pl.pallas_call(eliminate_kernel, out_shape=jax.ShapeDtypeStruct((RANK, sy...]
where the time goes in v5:
time: 72.9 us; the launch traced here: 72.8 us
  Pallas kernels  72.8 us (100%)
    pallas_call x1, Pallas kernels, normal_system(): pl.pallas_call(functools.partial(step_kernel, fib_size, pln_size), out_sh...  67.2 us
    pallas_call x1, Pallas kernels, eliminate(): pl.pallas_call(eliminate_kernel, out_shape=jax.ShapeDtypeStruct((RANK, sy...  5.54 us

profile of v5, /device:TPU:1, one launch (start us, length us, event | category | flops | bytes accessed | tf_op | source)
XLA Modules:
  0.0 72.8 jit_solution(11413013178491592094)
XLA Ops:
  0.0 67.2 %shard_map.55.system_ref = f32[128,256]{1,0:T(8,128)} custom-call(f32[288,1000]{1,0:T(8,128)} %bitcast.4, f32[1000,512]{1,0:T(8,128)} %interp_hbm.1, s32[3,1,64]{2,1,0:T(1,128)} %bitcast.5, s32[1,192]{1,0:T(1,128)} %bitcast.6, f32[768,128]{1,0:T(8,128)} %basis_hbm.1), custom_call_target="tpu_custom_call" | custom-call | tf_op jit(solution)/shard_map/pallas_call | solution.py:327
  67.2 5.5 %shard_map.56 = f32[128,128]{1,0:T(8,128)} custom-call(f32[128,256]{1,0:T(8,128)} %shard_map.55.system_ref), custom_call_target="tpu_custom_call" | custom-call | tf_op jit(solution)/shard_map/pallas_call | solution.py:67

commit v6 on v5

--- a/solution.py
+++ b/solution.py
@@ -110,6 +110,12 @@
     def other_core(self):
         return self.at_fib(self.chip * 2 + 1 - self.core)
 
+    def along_z(self, step):
+        return self.on_chip(lax.rem(self.z + step, self.depth) * X_CHIPS + self.x)
+
+    def along_x(self, step):
+        return self.on_chip(self.z * X_CHIPS + self.x_after[step])
+
     def after(self, distance):
         return lax.rem(self.fib + distance, self.fib_size)
 
@@ -162,7 +168,7 @@
                 nodes_ref, interp_ref, basis_ref, outgoing, incoming, brick, field_ref, image_ref, part, other,
                 half, chip_parts, chunk_sum, plane_parts, chunk_done, load_sems, shift_send, shift_recv,
                 tile_send, tile_recv, core_sems, chip_send, chip_recv, plane_send, plane_recv, gather_send,
-                gather_recv, relay_send, relay_recv):
+                gather_recv, relay_send, relay_recv, ready):
     at = Place(fib_size, pln_size)
     chips, planes = at.chips, at.planes
     size = PIECES // 2 // chips
@@ -176,8 +182,12 @@
     def greet(device):
         pl.semaphore_signal(barrier, inc=1, device_id=device, device_id_type=MESH_ID)
 
-    at.each_device(lambda i, fib: greet(at.at_fib(fib)), far_first=True)
-    loop(1, planes, lambda i: greet(at.in_plane(i)))
+    near = [at.along_z(1), at.along_z(at.depth - 1)], [at.along_x(1), at.along_x(X_CHIPS - 1)], [at.other_core()]
+    layers = [at.in_plane(1), at.in_plane(planes - 1)]
+    window = [at.at_fib(at.after(step)) for step in (1, 2, fib_size - 1, fib_size - 2)]
+    first = near[0] + near[1] + near[2] + layers + window
+    for device in first:
+        greet(device)
     for load in loads:
         load.start()
 
@@ -211,7 +221,7 @@
         else:
             outgoing[distance - 1] = values
             if distance == WINDOW - 1:
-                pl.semaphore_wait(barrier, fib_size + planes - 2)
+                pl.semaphore_wait(barrier, len(first))
             for copy in shift_copies(distance):
                 copy.start()
 
@@ -226,6 +236,18 @@
     chosen = jnp.sum(chosen, axis=1, keepdims=True).astype(jnp.int32)
     select = lax.broadcasted_iota(jnp.int32, (R_ELEM, WINDOW * CAP), 1) == chosen
     select = jnp.where(select, 1.0, 0.0).astype(jnp.bfloat16)
+
+    rounds = [near[0]] * (at.depth // 2) + [near[1]] * (X_CHIPS // 2) + [near[2]]
+    for turn, devices in enumerate(rounds):
+        pairs = [(turn, devices)]
+        if turn < planes // 2:
+            pairs.append((len(rounds) + turn, layers))
+        for slot, others in pairs:
+            for device in others:
+                pl.semaphore_signal(ready.at[slot], inc=1, device_id=device, device_id_type=MESH_ID)
+        for slot, others in pairs:
+            pl.semaphore_wait(ready.at[slot], len(others))
+
     for distance in range(WINDOW - 1, 0, -1):
         for copy in shift_copies(distance):
             copy.wait_recv()
@@ -247,16 +269,19 @@
     field_ref[own_pieces(at.fib)] = brick[own_pieces(at.fib)]
     loop(1, fib_size, lambda i: tile_copy(i, at.fib).wait_recv())
 
-    field = field_ref[...].reshape(NX, RANK)
-    product = jnp.dot(field, gram(field, basis_ref[...]), precision=HIGHEST,
-                      preferred_element_type=jnp.float32)
-    part[...] = product.reshape(PIECES, 4, RANK)
-
-    swap = remote(part.at[pl.ds((1 - at.core) * split, split)], other, core_sems.at[0], core_sems.at[1],
-                  at.other_core())
+    coefficients = gram(field_ref[...].reshape(NX, RANK), basis_ref[...])
+
+    def partial_image(core):
+        rows = field_ref[pl.ds(core * split, split)].reshape(NX // 2, RANK)
+        product = jnp.dot(rows, coefficients, precision=HIGHEST, preferred_element_type=jnp.float32)
+        return product.reshape(split, 4, RANK)
+
+    part[...] = partial_image(1 - at.core)
+    swap = remote(part, other, core_sems.at[0], core_sems.at[1], at.other_core())
     swap.start()
+    half[...] = partial_image(at.core)
     swap.wait()
-    half[...] = part[pl.ds(at.core * split, split)] + other[...]
+    half[...] += other[...]
 
     def chunk_copy(i, chip):
         return remote(half.at[pl.ds(chip * size, size)], chip_parts.at[i], chip_send.at[i], chip_recv.at[i],
@@ -333,12 +358,13 @@
             vmem(*nodes.shape), vmem(*interp.shape), vmem(*basis.shape),
             vmem(WINDOW - 1, CAP, 4 * RANK), vmem(WINDOW, CAP, 4 * RANK), vmem(PIECES, 4, RANK),
             vmem(PIECES, 4, RANK), vmem(PIECES, 4, RANK),
-            vmem(PIECES, 4, RANK), vmem(size * chips, 4, RANK), vmem(size * chips, 4, RANK),
+            vmem(size * chips, 4, RANK), vmem(size * chips, 4, RANK), vmem(size * chips, 4, RANK),
             vmem(chips, size, 4, RANK), vmem(size, 4, RANK), vmem(pln_size, size, 4, RANK),
             vmem(size, 4, RANK),
             dma(3), dma(WINDOW - 1, CUTS), dma(WINDOW - 1, CUTS), dma(fib_size), dma(fib_size),
             dma(2), dma(chips), dma(chips), dma(pln_size), dma(pln_size), dma(chips), dma(chips),
             dma(chips), dma(chips),
+            pltpu.SemaphoreType.REGULAR((fib_size // 2 // X_CHIPS // 2 + X_CHIPS // 2 + 1 + pln_size // 2,)),
         ],
         compiler_params=pltpu.CompilerParams(collective_id=0, has_side_effects=True),
     )(nodes, interp, table, order, basis)

time: 72.9 us -> 75.5 us (1.036)
  Pallas kernels: 72.8 us -> 75.3 us
    pallas_call x1, Pallas kernels: 67.2 us -> 69.8 us  [normal_system(): pl.pallas_call(functools.partial(step_kernel, fib_size, pln_size), out_sh...]
where the time goes in v6:
time: 75.5 us; the launch traced here: 75.3 us
  Pallas kernels  75.3 us (100%)
    pallas_call x1, Pallas kernels, normal_system(): pl.pallas_call(functools.partial(step_kernel, fib_size, pln_size), out_sh...  69.8 us
    pallas_call x1, Pallas kernels, eliminate(): pl.pallas_call(eliminate_kernel, out_shape=jax.ShapeDtypeStruct((RANK, sy...  5.54 us

profile of v6, /device:TPU:1, one launch (start us, length us, event | category | flops | bytes accessed | tf_op | source)
XLA Modules:
  0.0 75.3 jit_solution(13320223489976109620)
XLA Ops:
  0.0 69.8 %shard_map.55.system_ref = f32[128,256]{1,0:T(8,128)} custom-call(f32[288,1000]{1,0:T(8,128)} %bitcast.4, f32[1000,512]{1,0:T(8,128)} %interp_hbm.1, s32[3,1,64]{2,1,0:T(1,128)} %bitcast.5, s32[1,192]{1,0:T(1,128)} %bitcast.6, f32[768,128]{1,0:T(8,128)} %basis_hbm.1), custom_call_target="tpu_custom_call" | custom-call | tf_op jit(solution)/shard_map/pallas_call | solution.py:352
  69.8 5.5 %shard_map.56 = f32[128,128]{1,0:T(8,128)} custom-call(f32[128,256]{1,0:T(8,128)} %shard_map.55.system_ref), custom_call_target="tpu_custom_call" | custom-call | tf_op jit(solution)/shard_map/pallas_call | solution.py:67

commit v7 on v6

--- a/solution.py
+++ b/solution.py
@@ -131,13 +131,16 @@
             row(0, False)
             loop(1, self.depth, lambda n: row(n, True))
 
-    def each_chip(self, body, far_first=False):
-        def row(z_step, with_own):
+    def row_of_chips(self, body):
+        def row(z_step, with_own=True):
             ahead = lax.rem(self.z + z_step, self.depth) * X_CHIPS
             behind = lax.rem(self.z + self.depth - z_step, self.depth) * X_CHIPS
             for x_step in range(0 if with_own else 1, X_CHIPS):
                 body(z_step * X_CHIPS + x_step, ahead + self.x_after[x_step], behind + self.x_before[x_step])
-        self.over_depth(row, far_first)
+        return row
+
+    def each_chip(self, body, far_first=False):
+        self.over_depth(self.row_of_chips(body), far_first)
 
     def each_device(self, body, far_first=False):
         def row(z_step, with_own):
@@ -159,6 +162,16 @@
     return jnp.dot(left, right, preferred_element_type=jnp.float32)
 
 
+def mult3(left, right, contract=1):
+    dims = (((contract,), (0,)), ((), ()))
+    (left_high, left_low), (right_high, right_low) = pair(left), pair(right)
+
+    def product(a, b):
+        return lax.dot_general(a, b, dims, preferred_element_type=jnp.float32)
+
+    return product(left_high, right_high) + (product(left_high, right_low) + product(left_low, right_high))
+
+
 def gram(left, right):
     return lax.dot_general(left, right, (((0,), (0,)), ((), ())), precision=HIGHEST,
                            preferred_element_type=jnp.float32)
@@ -168,7 +181,7 @@
                 nodes_ref, interp_ref, basis_ref, outgoing, incoming, brick, field_ref, image_ref, part, other,
                 half, chip_parts, chunk_sum, plane_parts, chunk_done, load_sems, shift_send, shift_recv,
                 tile_send, tile_recv, core_sems, chip_send, chip_recv, plane_send, plane_recv, gather_send,
-                gather_recv, relay_send, relay_recv, ready):
+                gather_recv, relay_send, relay_recv, ready, direct_send, direct_recv):
     at = Place(fib_size, pln_size)
     chips, planes = at.chips, at.planes
     size = PIECES // 2 // chips
@@ -182,10 +195,12 @@
     def greet(device):
         pl.semaphore_signal(barrier, inc=1, device_id=device, device_id_type=MESH_ID)
 
-    near = [at.along_z(1), at.along_z(at.depth - 1)], [at.along_x(1), at.along_x(X_CHIPS - 1)], [at.other_core()]
-    layers = [at.in_plane(1), at.in_plane(planes - 1)]
+    reach_z, reach_y = at.depth // 4, planes // 4
+    near_z = [at.along_z(step) for n in range(reach_z, 0, -1) for step in (n, at.depth - n)]
+    near_y = [at.in_plane(step) for n in range(reach_y, 0, -1) for step in (n, planes - n)]
+    line_x = [at.along_x(step) for step in range(1, X_CHIPS)]
     window = [at.at_fib(at.after(step)) for step in (1, 2, fib_size - 1, fib_size - 2)]
-    first = near[0] + near[1] + near[2] + layers + window
+    first = near_z + near_y + line_x + window + [at.other_core()]
     for device in first:
         greet(device)
     for load in loads:
@@ -237,11 +252,7 @@
     select = lax.broadcasted_iota(jnp.int32, (R_ELEM, WINDOW * CAP), 1) == chosen
     select = jnp.where(select, 1.0, 0.0).astype(jnp.bfloat16)
 
-    rounds = [near[0]] * (at.depth // 2) + [near[1]] * (X_CHIPS // 2) + [near[2]]
-    for turn, devices in enumerate(rounds):
-        pairs = [(turn, devices)]
-        if turn < planes // 2:
-            pairs.append((len(rounds) + turn, layers))
+    for pairs in (((0, near_z[:2]), (1, near_y[:2])), ((2, line_x),), ((3, [at.other_core()]),)):
         for slot, others in pairs:
             for device in others:
                 pl.semaphore_signal(ready.at[slot], inc=1, device_id=device, device_id_type=MESH_ID)
@@ -269,12 +280,11 @@
     field_ref[own_pieces(at.fib)] = brick[own_pieces(at.fib)]
     loop(1, fib_size, lambda i: tile_copy(i, at.fib).wait_recv())
 
-    coefficients = gram(field_ref[...].reshape(NX, RANK), basis_ref[...])
+    coefficients = mult3(field_ref[...].reshape(NX, RANK), basis_ref[...], 0)
 
     def partial_image(core):
         rows = field_ref[pl.ds(core * split, split)].reshape(NX // 2, RANK)
-        product = jnp.dot(rows, coefficients, precision=HIGHEST, preferred_element_type=jnp.float32)
-        return product.reshape(split, 4, RANK)
+        return mult3(rows, coefficients).reshape(split, 4, RANK)
 
     part[...] = partial_image(1 - at.core)
     swap = remote(part, other, core_sems.at[0], core_sems.at[1], at.other_core())
@@ -318,7 +328,23 @@
     def relay_copy(i, source, chip):
         return remote(source, image_ref.at[place_of(chip)], relay_send.at[i], relay_recv.at[i], at.other_core())
 
-    at.each_chip(lambda i, chip, back: gather_copy(i, chip).start(), far_first=True)
+    far = at.depth // 2
+
+    def direct_copy(i, chip):
+        return remote(chunk_done, image_ref.at[place_of(at.chip)], direct_send.at[i], direct_recv.at[i],
+                      at.at_fib(chip * 2 + 1 - at.core))
+
+    def send_far(i, chip, back):
+        gather_copy(i, chip).start()
+        direct_copy(i - far * X_CHIPS, chip).start()
+
+    def other_rows(row):
+        loop(far + 1, at.depth, row)
+        loop(1, far, row)
+        row(0, False)
+
+    at.row_of_chips(send_far)(far)
+    other_rows(at.row_of_chips(lambda i, chip, back: gather_copy(i, chip).start()))
     relay_copy(0, chunk_done, at.chip).start()
     image_ref[place_of(at.chip)] = chunk_done[...]
 
@@ -326,12 +352,24 @@
         gather_copy(i, chip).wait_recv()
         relay_copy(i, image_ref.at[place_of(back)], back).start()
 
-    at.each_chip(pass_on)
-    loop(0, chips, lambda i: relay_copy(i, chunk_done, at.chip).wait())
-
-    image = image_ref[...].reshape(NX, RANK)
-    system_ref[:, :RANK] = gram(image, image)
-    system_ref[:, RANK:] = gram(image, field_ref[...].reshape(NX, RANK))
+    row = at.row_of_chips(pass_on)
+    row(0, False)
+    loop(1, far, row)
+    loop(far + 1, at.depth, row)
+    loop(far * X_CHIPS, (far + 1) * X_CHIPS, lambda i: gather_copy(i, at.chip).wait_recv())
+
+    def half_system(core):
+        image = image_ref[pl.ds(core * split, split)].reshape(NX // 2, RANK)
+        field = field_ref[pl.ds(core * split, split)].reshape(NX // 2, RANK)
+        return gram(image, image), mult3(image, field, 0)
+
+    own_normal, own_right = half_system(at.core)
+    for low, high in ((0, far * X_CHIPS), ((far + 1) * X_CHIPS, chips)):
+        loop(low, high, lambda i: relay_copy(i, chunk_done, at.chip).wait())
+    loop(0, X_CHIPS, lambda i: direct_copy(i, at.chip).wait())
+    other_normal, other_right = half_system(1 - at.core)
+    system_ref[:, :RANK] = own_normal + other_normal
+    system_ref[:, RANK:] = own_right + other_right
 
     loop(1, fib_size, lambda i: tile_copy(i, at.fib).wait_send())
     loop(1, chips, lambda i: chunk_copy(i, at.chip).wait_send())
@@ -364,7 +402,7 @@
             dma(3), dma(WINDOW - 1, CUTS), dma(WINDOW - 1, CUTS), dma(fib_size), dma(fib_size),
             dma(2), dma(chips), dma(chips), dma(pln_size), dma(pln_size), dma(chips), dma(chips),
             dma(chips), dma(chips),
-            pltpu.SemaphoreType.REGULAR((fib_size // 2 // X_CHIPS // 2 + X_CHIPS // 2 + 1 + pln_size // 2,)),
+            pltpu.SemaphoreType.REGULAR((4,)), dma(X_CHIPS), dma(X_CHIPS),
         ],
         compiler_params=pltpu.CompilerParams(collective_id=0, has_side_effects=True),
     )(nodes, interp, table, order, basis)

time: 75.5 us -> 71.7 us (0.950)
  Pallas kernels: 75.3 us -> 71.5 us
    pallas_call x1, Pallas kernels: 69.8 us -> 65.9 us  [normal_system(): pl.pallas_call(functools.partial(step_kernel, fib_size, pln_size), out_sh...]
where the time goes in v7:
time: 71.7 us; the launch traced here: 71.5 us
  Pallas kernels  71.5 us (100%)
    pallas_call x1, Pallas kernels, normal_system(): pl.pallas_call(functools.partial(step_kernel, fib_size, pln_size), out_sh...  65.9 us
    pallas_call x1, Pallas kernels, eliminate(): pl.pallas_call(eliminate_kernel, out_shape=jax.ShapeDtypeStruct((RANK, sy...  5.54 us

profile of v7, /device:TPU:1, one launch (start us, length us, event | category | flops | bytes accessed | tf_op | source)
XLA Modules:
  0.0 71.5 jit_solution(10706291204650728266)
XLA Ops:
  0.0 65.9 %shard_map.55.system_ref = f32[128,256]{1,0:T(8,128)} custom-call(f32[288,1000]{1,0:T(8,128)} %bitcast.4, f32[1000,512]{1,0:T(8,128)} %interp_hbm.1, s32[3,1,64]{2,1,0:T(1,128)} %bitcast.5, s32[1,192]{1,0:T(1,128)} %bitcast.6, f32[768,128]{1,0:T(8,128)} %basis_hbm.1), custom_call_target="tpu_custom_call" | custom-call | tf_op jit(solution)/shard_map/pallas_call | solution.py:390
  65.9 5.5 %shard_map.56 = f32[128,128]{1,0:T(8,128)} custom-call(f32[128,256]{1,0:T(8,128)} %shard_map.55.system_ref), custom_call_target="tpu_custom_call" | custom-call | tf_op jit(solution)/shard_map/pallas_call | solution.py:67

commit v8 on v7

--- a/solution.py
+++ b/solution.py
@@ -264,8 +264,7 @@
             copy.wait_recv()
     rows = incoming[...].reshape(WINDOW * CAP, 4 * RANK)
     high, low = pair(rows)
-    rest = (rows - high.astype(jnp.float32)) - low.astype(jnp.float32)
-    values = mult(select, high) + (mult(select, low) + mult(select, rest.astype(jnp.bfloat16)))
+    values = mult(select, high) + mult(select, low)
     for l in range(4):
         brick[:, l, :] = values[:, l * RANK:(l + 1) * RANK]
 

time: 71.7 us -> 71.5 us (level)
  no operation moved by 1% of the time
where the time goes in v8:
time: 71.5 us; the launch traced here: 71.4 us
  Pallas kernels  71.4 us (100%)
    pallas_call x1, Pallas kernels, normal_system(): pl.pallas_call(functools.partial(step_kernel, fib_size, pln_size), out_sh...  65.8 us
    pallas_call x1, Pallas kernels, eliminate(): pl.pallas_call(eliminate_kernel, out_shape=jax.ShapeDtypeStruct((RANK, sy...  5.54 us

profile of v8, /device:TPU:1, one launch (start us, length us, event | category | flops | bytes accessed | tf_op | source)
XLA Modules:
  0.0 71.4 jit_solution(9799685830040483243)
XLA Ops:
  0.0 65.8 %shard_map.55.system_ref = f32[128,256]{1,0:T(8,128)} custom-call(f32[288,1000]{1,0:T(8,128)} %bitcast.4, f32[1000,512]{1,0:T(8,128)} %interp_hbm.1, s32[3,1,64]{2,1,0:T(1,128)} %bitcast.5, s32[1,192]{1,0:T(1,128)} %bitcast.6, f32[768,128]{1,0:T(8,128)} %basis_hbm.1), custom_call_target="tpu_custom_call" | custom-call | tf_op jit(solution)/shard_map/pallas_call | solution.py:389
  65.8 5.5 %shard_map.56 = f32[128,128]{1,0:T(8,128)} custom-call(f32[128,256]{1,0:T(8,128)} %shard_map.55.system_ref), custom_call_target="tpu_custom_call" | custom-call | tf_op jit(solution)/shard_map/pallas_call | solution.py:67
